TPU v7x, 128 devices: a whole 4x4x4 slice. The times are simulated.
128 devices in a mesh: section: 2 (over x_hi), rows: 16 (over y, x_lo, core), cols: 4 (over z).
Axes of the slice: x: 4 (x_hi: 2, x_lo: 2; x = x_hi * 2 + x_lo), y: 4, z: 4, core: 2. Of those that a mesh axis runs over, the one named last changes fastest.
Arguments:
- features: bfloat16 [2, 384, 96, 728], P(None, ('rows', 'cols')), may hold values from -6 to 6
- upstream: bfloat16 [2, 384, 96, 256], P(None, 'rows', 'cols'), may hold values from -0.0234375 to 0.0234375
- depth_mid: float32 [9, 728], replicated, may hold values from -2 to 2
- point_mid: bfloat16 [728, 728], replicated, may hold values from -0.21875 to 0.21875
- projection: bfloat16 [728, 2048], replicated, may hold values from -0.21875 to 0.21875
- depth_first: float32 [9, 2048], replicated, may hold values from -2 to 2
- point_first: bfloat16 [2048, 256], replicated, may hold values from -0.125 to 0.125
- depth_later: float32 [2, 9, 256], replicated, may hold values from -2 to 2
- point_later: bfloat16 [2, 256, 256], replicated, may hold values from -0.375 to 0.375
- joining: bfloat16 [768, 256], replicated, may hold values from -0.21875 to 0.21875
- rate_first: int32 [2], replicated, may hold values from 1 to 6, as said below
- rates_later: int32 [2, 2], replicated, may hold values from 1 to 21, as said below
Outputs:
- grad_mid: float32 [728, 728], replicated
- grad_later: float32 [2, 256, 256], replicated
Inputs may be any that keep to these rules, and one draw needn't show every extreme that they name: `rate_first`: at least one of the two rates equals 6. `rates_later`: at least one of the rates equals 21.
All inputs are finite; a program needn't handle non-finite values.
Results may differ from a plain program's by a relative error of at most 0.015.
Values may be sent and summed in bfloat16 or wider, within the bound.
No kernel may reach another device: no remote copies, remote signals or barrier semaphores. Data moves between devices by JAX's collectives and lax.ppermute only.
A program may use at most 128 MiB of HBM per device.

v0:
```python
import jax
import jax.numpy as jnp
from jax import lax
from jax.experimental import pallas as pl
from jax.experimental.pallas import tpu as pltpu
from jax.sharding import Mesh, PartitionSpec as P

BF = jnp.bfloat16
F32 = jnp.float32
SLABS = ("y", "xl", "core", "z")
CHIPS = ("xh", "y", "xl", "z")
VM = pl.BlockSpec(memory_space=pltpu.VMEM)
SM = pl.BlockSpec(memory_space=pltpu.SMEM)
NN = (((1,), (0,)), ((), ()))
NT = (((1,), (1,)), ((), ()))
TN = (((0,), (0,)), ((), ()))


def mm(a, b, dims=NN):
    return lax.dot_general(a, b, dims, preferred_element_type=F32)


def sigmoid(v):
    return 1.0 / (1.0 + jnp.exp(-v))


def slope(v):
    s = sigmoid(v)
    return s * (1.0 + v * (1.0 - s))


def shifter(width, rate):
    j = lax.broadcasted_iota(jnp.int32, (2 * width, width), 0)
    c = lax.broadcasted_iota(jnp.int32, (2 * width, width), 1)
    want = jnp.where(j < width, j - rate, j - width + rate)
    return jnp.where(c == want, 1.0, 0.0).astype(BF)


def from_slab(value, shift, ring=False):
    count = lax.axis_size(SLABS)
    pairs = [(i, i - shift) for i in range(count) if 0 <= i - shift < count]
    if ring:
        pairs = [(i, (i - shift) % count) for i in range(count)]
    return lax.ppermute(value, SLABS, pairs)


def masked(window_ref, i, row, height):
    inside = jnp.logical_and(row + i >= 0, row + i < height)
    return window_ref[i] * jnp.where(inside, 1.0, 0.0).astype(BF)


def weights_kernel(proj_ref, point_ref, taps_ref, out_ref):
    n = point_ref.shape[1]
    taps = jnp.concatenate([taps_ref[...], jnp.zeros((7, taps_ref.shape[1]), F32)], axis=0).T
    for t in range(9):
        a, b = divmod(t, 3)
        scaled = (point_ref[...].astype(F32) * taps[:, t : t + 1]).astype(BF)
        out_ref[b, :, a * n : (a + 1) * n] = mm(proj_ref[...], scaled).astype(BF)


def fold_weights(projection, point_first, depth_first):
    c, ch = projection.shape
    b = point_first.shape[1]
    return pl.pallas_call(
        weights_kernel,
        in_specs=[VM] * 3,
        out_specs=VM,
        out_shape=jax.ShapeDtypeStruct((3, c, 3 * b), BF),
        cost_estimate=pl.CostEstimate(
            flops=18 * c * ch * b, bytes_accessed=8 * c * ch, transcendentals=0
        ),
        name="fold_weights",
    )(projection, point_first, depth_first)


def front_kernel(
    rate_ref, feat_ref, up_ref, dn_ref, taps_ref, point_ref, m_ref,
    mid_ref, u0_ref, above_ref, below_ref, act, so, left, right,
):
    part, rate = lax.axis_index("xh"), rate_ref[1]
    rows, width, c = feat_ref.shape[1:]
    zero = jnp.zeros((rows + 2, 8, c), F32)
    act[:, 0:8, :] = zero
    act[:, width + 8 : width + 16, :] = zero

    def activate(v):
        v = v.astype(F32)
        return v * sigmoid(v)

    act[0, 8 : width + 8, :] = activate(up_ref[...])
    act[rows + 1, 8 : width + 8, :] = activate(dn_ref[...])

    def fill(i, carry):
        act[i + 1, 8 : width + 8, :] = activate(feat_ref[part, i])
        return carry

    lax.fori_loop(0, rows, fill, 0)

    def conv(i, carry):
        at = pl.multiple_of(i * width, width)
        for lo in range(0, c, 128):
            hi = min(lo + 128, c)
            total = jnp.zeros((width, hi - lo), F32)
            for a in range(3):
                for b in range(3):
                    total = total + (
                        act[i + a, 7 + b : 7 + b + width, lo:hi]
                        * taps_ref[3 * a + b : 3 * a + b + 1, lo:hi]
                    )
            mid_ref[pl.ds(at, width), lo:hi] = total.astype(BF)
        return carry

    lax.fori_loop(0, rows, conv, 0)
    mixed = mm(mid_ref[...], point_ref[...])
    so[...] = (feat_ref[part].reshape(rows * width, c).astype(F32) + mixed).astype(BF)
    move = shifter(width, rate)

    def shift(i, carry):
        at = pl.ds(pl.multiple_of(i * width, width), width)
        moved = mm(move, so[at, :]).astype(BF)
        left[at, :] = moved[:width]
        right[at, :] = moved[width:]
        return carry

    lax.fori_loop(0, rows, shift, 0)
    n = u0_ref.shape[1]
    total = mm(left[...], m_ref[0]) + mm(so[...], m_ref[1]) + mm(right[...], m_ref[2])
    above_ref[...] = total[:, :n].astype(BF).reshape(rows, width, n)
    u0_ref[...] = total[:, n : 2 * n]
    below_ref[...] = total[:, 2 * n :].astype(BF).reshape(rows, width, n)


def front(rates, features, up, dn, depth_mid, point_mid, folded):
    _, rows, width, c = features.shape
    n = folded.shape[2] // 3
    cells = rows * width
    return pl.pallas_call(
        front_kernel,
        in_specs=[SM] + [VM] * 6,
        out_specs=[VM] * 4,
        out_shape=[
            jax.ShapeDtypeStruct((cells, c), BF),
            jax.ShapeDtypeStruct((cells, n), F32),
            jax.ShapeDtypeStruct((rows, width, n), BF),
            jax.ShapeDtypeStruct((rows, width, n), BF),
        ],
        scratch_shapes=[
            pltpu.VMEM((rows + 2, width + 16, c), F32),
            pltpu.VMEM((cells, c), BF),
            pltpu.VMEM((cells, c), BF),
            pltpu.VMEM((cells, c), BF),
        ],
        name="front",
    )(rates, features, up, dn, depth_mid, point_mid, folded)


def first_kernel(
    rate_ref, u0_ref, above_ref, below_ref, up_ref, dn_ref, pre_ref, out_ref, top_ref, end_ref
):
    rate = rate_ref[0]
    rows, width, n = out_ref.shape
    edge = rows // 2

    def one(i, carry):
        at = pl.ds(pl.multiple_of(i * width, width), width)
        high, low = i - rate, i + rate
        inner = above_ref[jnp.maximum(high, 0)].astype(F32)
        outer = up_ref[jnp.minimum(high + rows, rows - 1)].astype(F32)
        total = u0_ref[at, :] + jnp.where(high >= 0, inner, outer)
        inner = below_ref[jnp.minimum(low, rows - 1)].astype(F32)
        outer = dn_ref[jnp.maximum(low - rows, 0)].astype(F32)
        total = total + jnp.where(low < rows, inner, outer)
        pre_ref[at, :] = total
        out_ref[i] = (total * sigmoid(total)).astype(BF)
        return carry

    lax.fori_loop(0, rows, one, 0)
    top_ref[...] = out_ref[:edge]
    end_ref[...] = out_ref[rows - edge :]


def first(rates, u0, above, below, up, dn):
    rows, width, n = above.shape
    edge = rows // 2
    return pl.pallas_call(
        first_kernel,
        in_specs=[SM] + [VM] * 5,
        out_specs=[VM] * 4,
        out_shape=[
            jax.ShapeDtypeStruct((rows * width, n), F32),
            jax.ShapeDtypeStruct((rows, width, n), BF),
            jax.ShapeDtypeStruct((edge, width, n), BF),
            jax.ShapeDtypeStruct((edge, width, n), BF),
        ],
        name="first",
    )(rates, u0, above, below, up, dn)


def cut_kernel(sc_ref, up_ref, own_ref, dn_ref, p0_ref, m0_ref, p1_ref, m1_ref):
    many, rows, width, n = own_ref.shape
    edge = rows // 2
    outs = ((p0_ref, m0_ref), (p1_ref, m1_ref))

    def one(i, carry):
        for l in range(2):
            k = l % many
            rate = sc_ref[l, 0]
            rest = rate - (rate + edge - 1) // rows * rows
            for sign in (1, -1):
                j = i + sign * rest
                near = own_ref[k, jnp.clip(j, 0, rows - 1)]
                far = dn_ref[k, jnp.clip(j - rows, 0, edge - 1)]
                back = up_ref[k, jnp.clip(j + edge, 0, edge - 1)]
                row = jnp.where(j < 0, back, jnp.where(j < rows, near, far))
                outs[l][(1 - sign) // 2][i] = row
        return carry

    lax.fori_loop(0, rows, one, 0)


def cut(rates, up, own, dn):
    _, rows, width, n = own.shape
    return pl.pallas_call(
        cut_kernel,
        in_specs=[SM] + [VM] * 3,
        out_specs=[VM] * 4,
        out_shape=[jax.ShapeDtypeStruct((rows, width, n), BF)] * 4,
        name="cut",
    )(rates, up, own, dn)


def later_kernel(
    sc_ref, own_ref, p0_ref, m0_ref, p1_ref, m1_ref, up_ref, join_ref, taps_ref, point_ref,
    back_ref, top_ref, end_ref, grad_ref, direct_ref, conv,
):
    rows, width, n = own_ref.shape
    first, height = lax.axis_index(SLABS) * rows, lax.axis_size(SLABS) * rows
    windows = ((m0_ref, own_ref, p0_ref), (m1_ref, own_ref, p1_ref))
    for l in range(2):
        move = shifter(width, sc_ref[l, 1])

        def one(i, carry, l=l, move=move):
            total = jnp.zeros((width, n), F32)
            for a in range(3):
                row = masked(windows[l][a], i, first + (a - 1) * sc_ref[l, 0], height)
                moved = mm(move, row)
                total = total + moved[:width] * taps_ref[l, 3 * a : 3 * a + 1, :]
                total = total + row.astype(F32) * taps_ref[l, 3 * a + 1 : 3 * a + 2, :]
                total = total + moved[width:] * taps_ref[l, 3 * a + 2 : 3 * a + 3, :]
            conv[pl.ds(pl.multiple_of(i * width, width), width), :] = total.astype(BF)
            return carry

        lax.fori_loop(0, rows, one, 0)
        pre = mm(conv[...], point_ref[l])
        block = mm(up_ref[...], join_ref[(l + 1) * n : (l + 2) * n, :], NT)
        gate = (block * slope(pre)).astype(BF)
        back = mm(gate, point_ref[l], NT).astype(BF)
        back = back.reshape(rows, width, n)
        back_ref[l] = back
        top_ref[l] = back[: rows // 2]
        end_ref[l] = back[rows - rows // 2 :]
        grad_ref[l] = mm(conv[...], gate, TN)
    direct_ref[...] = mm(up_ref[...], join_ref[:n, :], NT)


def later(rates, own, windows, upstream, joining, depth, point):
    rows, width, n = own.shape
    cells = rows * width
    return pl.pallas_call(
        later_kernel,
        in_specs=[SM] + [VM] * 9,
        out_specs=[VM] * 5,
        out_shape=[
            jax.ShapeDtypeStruct((2, rows, width, n), BF),
            jax.ShapeDtypeStruct((2, rows // 2, width, n), BF),
            jax.ShapeDtypeStruct((2, rows // 2, width, n), BF),
            jax.ShapeDtypeStruct((2, n, n), F32),
            jax.ShapeDtypeStruct((cells, n), F32),
        ],
        scratch_shapes=[pltpu.VMEM((cells, n), BF)],
        name="later",
    )(rates, own, *windows, upstream, joining, depth, point)


def gate_kernel(
    sc_ref, own_ref, p0_ref, m0_ref, p1_ref, m1_ref, direct_ref, pre_ref, taps_ref, out_ref
):
    _, rows, width, n = own_ref.shape
    first, height = lax.axis_index(SLABS) * rows, lax.axis_size(SLABS) * rows
    windows = ((p0_ref, own_ref.at[0], m0_ref), (p1_ref, own_ref.at[1], m1_ref))
    moves = [shifter(width, sc_ref[l, 1]) for l in range(2)]

    def one(i, carry):
        at = pl.ds(pl.multiple_of(i * width, width), width)
        total = direct_ref[at, :]
        for l in range(2):
            for a in range(3):
                row = masked(windows[l][a], i, first - (a - 1) * sc_ref[l, 0], height)
                moved = mm(moves[l], row)
                total = total + moved[width:] * taps_ref[l, 3 * a : 3 * a + 1, :]
                total = total + row.astype(F32) * taps_ref[l, 3 * a + 1 : 3 * a + 2, :]
                total = total + moved[:width] * taps_ref[l, 3 * a + 2 : 3 * a + 3, :]
        out_ref[i] = (total * slope(pre_ref[at, :])).astype(BF)
        return carry

    lax.fori_loop(0, rows, one, 0)


def gate(rates, back, windows, direct, pre, depth):
    return pl.pallas_call(
        gate_kernel,
        in_specs=[SM] + [VM] * 8,
        out_specs=VM,
        out_shape=jax.ShapeDtypeStruct(back.shape[1:], BF),
        name="gate",
    )(rates, back, *windows, direct, pre, depth)


def grads_kernel(
    sc_ref, up_ref, own_ref, dn_ref, mid_ref, m_ref, later_ref, keep_ref, give_ref,
    g0, g1, g2, back,
):
    rate_row, rate_col = sc_ref[0], sc_ref[1]
    rows, width, n = own_ref.shape
    c = mid_ref.shape[1]
    move = shifter(width, rate_col)

    def one(i, carry):
        at = pl.ds(pl.multiple_of(i * width, width), width)
        for a in range(3):
            j = i - (a - 1) * rate_row
            row = own_ref[jnp.clip(j, 0, rows - 1)]
            if a == 0:
                row = jnp.where(j < rows, row, dn_ref[jnp.maximum(j - rows, 0)])
            if a == 2:
                row = jnp.where(j >= 0, row, up_ref[jnp.minimum(j + rows, rows - 1)])
            moved = mm(move, row).astype(BF)
            g0[at, a * n : (a + 1) * n] = moved[width:]
            g1[at, a * n : (a + 1) * n] = row
            g2[at, a * n : (a + 1) * n] = moved[:width]
        return carry

    lax.fori_loop(0, rows, one, 0)
    total = mm(g0[...], m_ref[0], NT) + mm(g1[...], m_ref[1], NT) + mm(g2[...], m_ref[2], NT)
    back[...] = total.astype(BF)
    core = lax.axis_index("core")

    def put(k, lo, hi, wide, value):
        @pl.when(core == k // 2)
        def _():
            keep_ref[k % 2, lo:hi, :wide] = value

        @pl.when(core != k // 2)
        def _():
            give_ref[k % 2, lo:hi, :wide] = value.astype(BF)

    keep_ref[:, c:, :] = jnp.zeros((2, keep_ref.shape[1] - c, n), F32)
    give_ref[:, c:, :] = jnp.zeros((2, keep_ref.shape[1] - c, n), BF)
    for k in range(3):
        lo, hi = k * n, min((k + 1) * n, c)
        part = mm(mid_ref[...], back[:, lo:hi], TN)
        if hi - lo < n:
            part = jnp.concatenate([part, jnp.zeros((c, n - hi + lo), F32)], axis=1)
        put(k, 0, c, n, part)
    for l in range(2):
        put(3, l * n, (l + 1) * n, n, later_ref[l])
    put(3, 2 * n, c, n, jnp.zeros((c - 2 * n, n), F32))


def grads(rates, up, own, dn, mid, folded, later_grads):
    cells, c = mid.shape
    n = own.shape[2]
    return pl.pallas_call(
        grads_kernel,
        in_specs=[SM] + [VM] * 6,
        out_specs=[VM] * 2,
        out_shape=[
            jax.ShapeDtypeStruct((2, 3 * n, n), F32),
            jax.ShapeDtypeStruct((2, 3 * n, n), BF),
        ],
        scratch_shapes=[pltpu.VMEM((cells, 3 * n), BF)] * 3 + [pltpu.VMEM((cells, c), BF)],
        name="grads",
    )(rates, up, own, dn, mid, folded, later_grads)


def row_windows(own, top, end, rates):
    rows = own.shape[1]
    below = from_slab(top, 1, ring=True)
    above = from_slab(end, -1, ring=True)
    p0, m0, p1, m1 = cut(rates, above, own, below)
    whole = (rates[:, 0] + rows // 2 - 1) // rows

    def at(q):
        def fetch(plus, minus):
            if q == 0:
                return plus, minus
            return from_slab(plus, q, ring=True), from_slab(minus, -q, ring=True)

        return fetch

    cases = [at(q) for q in range(4)]
    return lax.switch(whole[0], cases, p0, m0) + lax.switch(whole[1], cases, p1, m1)


def total_over_devices(keep, give):
    core = lax.axis_index("core")
    swap = [(0, 1), (1, 0)]
    half, rows, lanes = keep.shape
    chips = lax.axis_size(CHIPS)
    mine = (keep + lax.ppermute(give, "core", swap).astype(F32)).astype(BF)
    mine = mine.reshape(chips, half * rows // chips, lanes)

    def swapped(pieces):
        return lax.all_to_all(pieces, CHIPS, split_axis=0, concat_axis=0, tiled=True)

    piece = jnp.sum(swapped(mine).astype(F32), axis=0).astype(BF)
    whole = swapped(jnp.broadcast_to(piece[None], mine.shape)).reshape(half, rows, lanes)
    other = lax.ppermute(whole, "core", swap)
    first = jnp.where(core == 0, whole, other)
    second = jnp.where(core == 0, other, whole)
    return jnp.concatenate([first, second])


def local(
    features, upstream, depth_mid, point_mid, projection, depth_first, point_first,
    depth_later, point_later, joining, rate_first, rates_later,
):
    part = lax.axis_index("xh")
    _, rows, width, c = features.shape
    n = point_later.shape[1]
    cells = rows * width
    groups = lax.axis_size("z")
    down = from_slab(features[part, 0], 1)
    up = from_slab(features[part, rows - 1], -1)
    folded = fold_weights(projection, point_first, depth_first)
    tile = upstream[part].reshape(groups, rows, width // groups, n)
    slab = lax.all_to_all(tile, "z", split_axis=0, concat_axis=0, tiled=True)
    slab = slab.transpose(1, 0, 2, 3).reshape(cells, n)

    up, down, slab = lax.optimization_barrier((up, down, slab))
    mid, u0, above, below = front(
        rate_first, features, up, down, depth_mid, point_mid, folded
    )
    from_up = from_slab(above, -1)
    from_down = from_slab(below, 1)
    first_pre, first_out, top, end = first(rate_first, u0, above, below, from_up, from_down)
    windows = row_windows(first_out[None], top[None], end[None], rates_later)
    back, top, end, later_grads, direct = later(
        rates_later, first_out, windows, slab, joining, depth_later, point_later
    )
    windows = row_windows(back, top, end, rates_later)
    gated = gate(rates_later, back, windows, direct, first_pre, depth_later)
    keep, give = grads(
        rate_first, from_slab(gated, -1), gated, from_slab(gated, 1), mid, folded, later_grads
    )
    total = total_over_devices(keep, give).astype(F32)
    grad_mid = jnp.concatenate([total[0], total[1], total[2]], axis=1)[:c, :c]
    return grad_mid, total[3, : 2 * n].reshape(2, n, n)


def solution(mesh):
    section, rows, cols = mesh.devices.shape
    fine = Mesh(
        mesh.devices.reshape(section, rows // 4, 2, 2, cols), ("xh", "y", "xl", "core", "z")
    ) if hasattr(mesh, "devices") else mesh
    placed = (
        P(None, SLABS, None, None),
        P(None, ("y", "xl", "core"), "z", None),
    ) + (P(),) * 10
    return jax.shard_map(local, mesh=fine, in_specs=placed, out_specs=(P(), P()), check_vma=False)
```

profile of v0, /device:TPU:1, one launch (start us, length us, event | category | flops | bytes accessed | tf_op | source)
XLA Modules:
  0.0 196.9 jit_solution(657180040962363074)
XLA Ops:
  2.4 5.8 %all-to-all-start = ((bf16[4,6,24,256]{3,2,1,0:T(8,128)(2,1)}), bf16[4,6,24,256]{3,2,1,0:T(8,128)(2,1)S(1)}, u32[]{:S(2)}, u32[]{:S(2)}) async-start(bf16[4,6,24,256]{3,2,1,0:T(8,128)(2,1)} %bitcast.2), calls=%async_computation | async-start | bytes 589824 | tf_op jit(solution)/shard_map/all_to_all | solution.py:437
  9.3 5.7 %collective-permute-start.25 = (bf16[96,728]{1,0:T(8,128)(2,1)S(1)}, bf16[96,728]{1,0:T(8,128)(2,1)S(1)}, u32[]{:S(2)}, u32[]{:S(2)}) collective-permute-start(bf16[96,728]{1,0:T(8,128)(2,1)S(1)} %get-tuple-element.161), channel_id=1, source_target_pairs={{1,0},{2,1},{3,2},{4,3},{5,4},{6,5},{7,6},{8,7},{9,8},{10,9},{11,1... | collective-permute-start | bytes 419336 | tf_op jit(solution)/shard_map/ppermute | solution.py:44
  15.0 1.9 collective-permute-start.24
  16.9 11.3 %fold_weights.1.m_ref = bf16[3,728,768]{2,1,0:T(8,128)(2,1)} custom-call(bf16[728,2048]{1,0:T(8,128)(2,1)} %proj_ref.1, bf16[2048,256]{1,0:T(8,128)(2,1)} %point_ref.3, f32[9,2048]{1,0:T(8,128)} %taps_ref.4), custom_call_target="tpu_custom_call" | custom-call | flops 6870269952 | bytes 11927552 | tf_op jit(solution)/shard_map/fold_weights/pallas_call | solution.py:64
  29.7 11.4 %front.1 = (bf16[576,728]{1,0:T(8,128)(2,1)}, f32[576,256]{1,0:T(8,128)}, bf16[6,96,256]{2,1,0:T(8,128)(2,1)}, bf16[6,96,256]{2,1,0:T(8,128)(2,1)}) custom-call(s32[2]{0:T(128)} %sc_ref.9, bf16[2,6,96,728]{3,2,1,0:T(8,128)(2,1)} %feat_ref.1, bf16[96,728]{1,0:T(8,128)(2,1)} %copy-done.10, bf16[96,728]{1,0:T(8,128)(2,1)} %copy-done.9, f32[9,728]{1,0:T(8,128)} %taps_ref.5, ...), custom_call_target="tpu_custom_call" | custom-call | tf_op jit(solution)/shard_map/front/pallas_call | solution.py:137
  41.1 1.9 collective-permute-start.26
  43.0 4.9 %collective-permute-start.27 = (bf16[6,96,256]{2,1,0:T(8,128)(2,1)}, bf16[6,96,256]{2,1,0:T(8,128)(2,1)S(1)}, u32[]{:S(2)}, u32[]{:S(2)}) collective-permute-start(bf16[6,96,256]{2,1,0:T(8,128)(2,1)} %get-tuple-element.128.below_ref), channel_id=1, source_target_pairs={{1,0},{2,1},{3,2},{4,3},{5,4},{6,5},{7,6},{8,7},{9,8},{10,9},{11,1... | collective-permute-start | bytes 884744 | tf_op jit(solution)/shard_map/ppermute | solution.py:44
  48.1 2.4 %collective-permute-done.26.up_ref = bf16[6,96,256]{2,1,0:T(8,128)(2,1)S(1)} collective-permute-done((bf16[6,96,256]{2,1,0:T(8,128)(2,1)}, bf16[6,96,256]{2,1,0:T(8,128)(2,1)S(1)}, u32[]{:S(2)}, u32[]{:S(2)}) %collective-permute-start.26) | collective-permute-done | bytes 294944 | tf_op jit(solution)/shard_map/ppermute | solution.py:44
  50.5 4.4 %collective-permute-done.27.dn_ref = bf16[6,96,256]{2,1,0:T(8,128)(2,1)S(1)} collective-permute-done((bf16[6,96,256]{2,1,0:T(8,128)(2,1)}, bf16[6,96,256]{2,1,0:T(8,128)(2,1)S(1)}, u32[]{:S(2)}, u32[]{:S(2)}) %collective-permute-start.27) | collective-permute-done | bytes 294944 | tf_op jit(solution)/shard_map/ppermute | solution.py:44
  55.7 2.8 %first.1 = (f32[576,256]{1,0:T(8,128)}, bf16[6,96,256]{2,1,0:T(8,128)(2,1)}, bf16[3,96,256]{2,1,0:T(8,128)(2,1)}, bf16[3,96,256]{2,1,0:T(8,128)(2,1)}) custom-call(s32[2]{0:T(128)} %sc_ref.9, f32[576,256]{1,0:T(8,128)} %get-tuple-element.126.u0_ref, bf16[6,96,256]{2,1,0:T(8,128)(2,1)} %get-tuple-element.127.above_ref, ...), custom_call_target="tpu_custom_call" | custom-call | tf_op jit(solution)/shard_map/first/pallas_call | solution.py:185
  58.5 3.6 %collective-permute-start.29 = (bf16[1,3,96,256]{3,2,1,0:T(8,128)(2,1)}, bf16[1,3,96,256]{3,2,1,0:T(8,128)(2,1)S(1)}, u32[]{:S(2)}, u32[]{:S(2)}) collective-permute-start(bf16[1,3,96,256]{3,2,1,0:T(8,128)(2,1)} %bitcast.32), channel_id=1, source_target_pairs={{0,63},{1,0},{2,1},{3,2},{4,3},{5,4},{6,5},{7,6},{8,7},{9,8},{10,9... | collective-permute-start | bytes 442376 | tf_op jit(solution)/shard_map/ppermute | solution.py:44
  65.2 2.9 %collective-permute-done.28.up_ref = bf16[1,3,96,256]{3,2,1,0:T(8,128)(2,1)S(1)} collective-permute-done((bf16[1,3,96,256]{3,2,1,0:T(8,128)(2,1)}, bf16[1,3,96,256]{3,2,1,0:T(8,128)(2,1)S(1)}, u32[]{:S(2)}, u32[]{:S(2)}) %collective-permute-start.28) | collective-permute-done | bytes 147488 | tf_op jit(solution)/shard_map/ppermute | solution.py:44
  70.4 11.4 %conditional.5 = ((bf16[6,96,256]{2,1,0:T(8,128)(2,1)S(1)}, bf16[6,96,256]{2,1,0:T(8,128)(2,1)S(1)})) conditional(s32[]{:T(128)} %bitcast.9, (bf16[6,96,256]{2,1,0:T(8,128)(2,1)S(1)}, bf16[6,96,256]{2,1,0:T(8,128)(2,1)S(1)}) %tuple.71, (bf16[6,96,256]{2,1,0:T(8,128)(2,1)S(1)}, ...), branch_computations={%region_4.5_spmd, %region_5.6_spmd, %region_6.7_spmd, %region_7.8_... | conditional | bytes 3539048 | solution.py:402
  72.0 7.0 %collective-permute-done.6 = bf16[6,96,256]{2,1,0:T(8,128)(2,1)S(1)} collective-permute-done((bf16[6,96,256]{2,1,0:T(8,128)(2,1)S(1)}, bf16[6,96,256]{2,1,0:T(8,128)(2,1)S(1)}, u32[]{:S(2)}, u32[]{:S(2)}) %collective-permute-start.6) | collective-permute-done | bytes 294944 | tf_op jit(solution)/shard_map/cond/branch_1_fun/ppermute | solution.py:44
  79.0 2.8 %collective-permute-done.7 = bf16[6,96,256]{2,1,0:T(8,128)(2,1)S(1)} collective-permute-done((bf16[6,96,256]{2,1,0:T(8,128)(2,1)S(1)}, bf16[6,96,256]{2,1,0:T(8,128)(2,1)S(1)}, u32[]{:S(2)}, u32[]{:S(2)}) %collective-permute-start.7) | collective-permute-done | bytes 294944 | tf_op jit(solution)/shard_map/cond/branch_1_fun/ppermute | solution.py:44
  81.8 6.5 %later.1 = (bf16[2,6,96,256]{3,2,1,0:T(8,128)(2,1)}, bf16[2,3,96,256]{3,2,1,0:T(8,128)(2,1)}, bf16[2,3,96,256]{3,2,1,0:T(8,128)(2,1)}, f32[2,256,256]{2,1,0:T(8,128)}, f32[576,256]{1,0:T(8,128)}) custom-call(s32[2,2]{1,0:T(2,128)} %sc_ref.8, bf16[6,96,256]{2,1,0:T(8,128)(2,1)} %get-tuple-element.129.own_ref, ...), custom_call_target="tpu_custom_call" | custom-call | tf_op jit(solution)/shard_map/later/pallas_call | solution.py:269
  88.3 3.0 %collective-permute-start.31 = (bf16[2,3,96,256]{3,2,1,0:T(8,128)(2,1)}, bf16[2,3,96,256]{3,2,1,0:T(8,128)(2,1)S(1)}, u32[]{:S(2)}, u32[]{:S(2)}) collective-permute-start(bf16[2,3,96,256]{3,2,1,0:T(8,128)(2,1)} %get-tuple-element.143), channel_id=1, source_target_pairs={{0,63},{1,0},{2,1},{3,2},{4,3},{5,4},{6,5},{7,6},{8,7},{9,8},{10,9... | collective-permute-start | bytes 884744 | tf_op jit(solution)/shard_map/ppermute | solution.py:44
  91.2 7.8 %collective-permute-done.30.up_ref = bf16[2,3,96,256]{3,2,1,0:T(8,128)(2,1)S(1)} collective-permute-done((bf16[2,3,96,256]{3,2,1,0:T(8,128)(2,1)}, bf16[2,3,96,256]{3,2,1,0:T(8,128)(2,1)S(1)}, u32[]{:S(2)}, u32[]{:S(2)}) %collective-permute-start.30) | collective-permute-done | bytes 294944 | tf_op jit(solution)/shard_map/ppermute | solution.py:44
  101.4 9.5 %conditional.7 = ((bf16[6,96,256]{2,1,0:T(8,128)(2,1)S(1)}, bf16[6,96,256]{2,1,0:T(8,128)(2,1)S(1)})) conditional(s32[]{:T(128)} %bitcast.9, (bf16[6,96,256]{2,1,0:T(8,128)(2,1)S(1)}, bf16[6,96,256]{2,1,0:T(8,128)(2,1)S(1)}) %tuple.73, (bf16[6,96,256]{2,1,0:T(8,128)(2,1)S(1)}, ...), branch_computations={%region_12.13_spmd, %region_13.14_spmd, %region_14.15_spmd, %regio... | conditional | bytes 3539048 | solution.py:402
  103.3 5.8 %collective-permute-done.18 = bf16[6,96,256]{2,1,0:T(8,128)(2,1)S(1)} collective-permute-done((bf16[6,96,256]{2,1,0:T(8,128)(2,1)S(1)}, bf16[6,96,256]{2,1,0:T(8,128)(2,1)S(1)}, u32[]{:S(2)}, u32[]{:S(2)}) %collective-permute-start.18) | collective-permute-done | bytes 294944 | tf_op jit(solution)/shard_map/cond/branch_1_fun/ppermute | solution.py:44
  110.9 4.2 %gate.1.own_ref = bf16[6,96,256]{2,1,0:T(8,128)(2,1)} custom-call(s32[2,2]{1,0:T(2,128)} %sc_ref.8, bf16[2,6,96,256]{3,2,1,0:T(8,128)(2,1)} %get-tuple-element.141.own_ref, bf16[6,96,256]{2,1,0:T(8,128)(2,1)S(1)} %get-tuple-element.146.p0_ref, bf16[6,96,256]{2,1,0:T(8,128)(2,1)S(1)} %get-tuple-element.147.m0_ref, ...), custom_call_target="tpu_custom_call" | custom-call | tf_op jit(solution)/shard_map/gate/pallas_call | solution.py:310
  115.1 2.9 %collective-permute-start.33 = (bf16[6,96,256]{2,1,0:T(8,128)(2,1)}, bf16[6,96,256]{2,1,0:T(8,128)(2,1)S(1)}, u32[]{:S(2)}, u32[]{:S(2)}) collective-permute-start(bf16[6,96,256]{2,1,0:T(8,128)(2,1)} %gate.1.own_ref), channel_id=1, source_target_pairs={{1,0},{2,1},{3,2},{4,3},{5,4},{6,5},{7,6},{8,7},{9,8},{10,9},{11,1... | collective-permute-start | bytes 884744 | tf_op jit(solution)/shard_map/ppermute | solution.py:44
  118.1 2.3 %collective-permute-start.32 = (bf16[6,96,256]{2,1,0:T(8,128)(2,1)}, bf16[6,96,256]{2,1,0:T(8,128)(2,1)S(1)}, u32[]{:S(2)}, u32[]{:S(2)}) collective-permute-start(bf16[6,96,256]{2,1,0:T(8,128)(2,1)} %gate.1.own_ref), channel_id=1, source_target_pairs={{0,1},{1,2},{2,3},{3,4},{4,5},{5,6},{6,7},{7,8},{8,9},{9,10},{10,1... | collective-permute-start | bytes 884744 | tf_op jit(solution)/shard_map/ppermute | solution.py:44
  120.4 2.6 %collective-permute-done.33.dn_ref = bf16[6,96,256]{2,1,0:T(8,128)(2,1)S(1)} collective-permute-done((bf16[6,96,256]{2,1,0:T(8,128)(2,1)}, bf16[6,96,256]{2,1,0:T(8,128)(2,1)S(1)}, u32[]{:S(2)}, u32[]{:S(2)}) %collective-permute-start.33) | collective-permute-done | bytes 294944 | tf_op jit(solution)/shard_map/ppermute | solution.py:44
  123.0 4.5 %collective-permute-done.32.up_ref = bf16[6,96,256]{2,1,0:T(8,128)(2,1)S(1)} collective-permute-done((bf16[6,96,256]{2,1,0:T(8,128)(2,1)}, bf16[6,96,256]{2,1,0:T(8,128)(2,1)S(1)}, u32[]{:S(2)}, u32[]{:S(2)}) %collective-permute-start.32) | collective-permute-done | bytes 294944 | tf_op jit(solution)/shard_map/ppermute | solution.py:44
  128.3 9.9 %grads.1 = (f32[2,768,256]{2,1,0:T(8,128)}, bf16[2,768,256]{2,1,0:T(8,128)(2,1)}) custom-call(s32[2]{0:T(128)} %sc_ref.9, bf16[6,96,256]{2,1,0:T(8,128)(2,1)} %copy-done.2, bf16[6,96,256]{2,1,0:T(8,128)(2,1)} %gate.1.own_ref, bf16[6,96,256]{2,1,0:T(8,128)(2,1)} %copy-done.1, bf16[576,728]{1,0:T(8,128)(2,1)} %get-tuple-element.154.mid_ref, ...), custom_call_target="tpu_custom_call" | custom-call | tf_op jit(solution)/shard_map/grads/pallas_call | solution.py:373
  138.2 3.2 %collective-permute-start.34 = (bf16[2,768,256]{2,1,0:T(8,128)(2,1)}, bf16[2,768,256]{2,1,0:T(8,128)(2,1)S(1)}, u32[]{:S(2)}, u32[]{:S(2)}) collective-permute-start(bf16[2,768,256]{2,1,0:T(8,128)(2,1)} %get-tuple-element.157), channel_id=1, source_target_pairs={{0,4},{4,0},{1,5},{5,1},{2,6},{6,2},{3,7},{7,3},{8,12},{12,8},{9,1... | collective-permute-start | bytes 2359304 | tf_op jit(solution)/shard_map/ppermute | solution.py:410
  141.4 2.1 %collective-permute-done.34 = bf16[2,768,256]{2,1,0:T(8,128)(2,1)S(1)} collective-permute-done((bf16[2,768,256]{2,1,0:T(8,128)(2,1)}, bf16[2,768,256]{2,1,0:T(8,128)(2,1)S(1)}, u32[]{:S(2)}, u32[]{:S(2)}) %collective-permute-start.34) | collective-permute-done | bytes 786464 | tf_op jit(solution)/shard_map/ppermute | solution.py:410
  145.2 25.2 %all_to_all.15 = bf16[64,24,256]{2,1,0:T(8,128)(2,1)S(1)} all-to-all(bf16[64,24,256]{2,1,0:T(8,128)(2,1)S(1)} %bitcast.24), channel_id=1, replica_groups=mesh['xh'=2,'y'=4,'xl'=2,'core'=2,'z'=4] {'xh','y','xl','z'}, dimensions={0} | all-to-all | bytes 1572864 | tf_op jit(solution)/shard_map/all_to_all | solution.py:414
  170.6 18.5 %all_to_all.16 = bf16[64,24,256]{2,1,0:T(8,128)(2,1)S(1)} all-to-all(bf16[64,24,256]{2,1,0:T(8,128)(2,1)S(1)} %broadcast_in_dim.18), channel_id=1, replica_groups=mesh['xh'=2,'y'=4,'xl'=2,'core'=2,'z'=4] {'xh','y','xl','z'}, dimensions={0} | all-to-all | bytes 1572864 | tf_op jit(solution)/shard_map/all_to_all | solution.py:414
  189.1 3.1 %collective-permute-start.35 = (bf16[2,768,256]{2,1,0:T(8,128)(2,1)S(1)}, bf16[2,768,256]{2,1,0:T(8,128)(2,1)S(1)}, u32[]{:S(2)}, u32[]{:S(2)}) collective-permute-start(bf16[2,768,256]{2,1,0:T(8,128)(2,1)S(1)} %bitcast.25), channel_id=1, source_target_pairs={{0,4},{4,0},{1,5},{5,1},{2,6},{6,2},{3,7},{7,3},{8,12},{12,8},{9,1... | collective-permute-start | bytes 2359304 | tf_op jit(solution)/shard_map/ppermute | solution.py:418
  192.2 1.9 collective-permute-done.35
  (62 shorter events, 22.0 us)
Async XLA Ops:
  0.6 1.1 copy-start
  2.4 25.8 %all-to-all-start = ((bf16[4,6,24,256]{3,2,1,0:T(8,128)(2,1)}), bf16[4,6,24,256]{3,2,1,0:T(8,128)(2,1)S(1)}, u32[]{:S(2)}, u32[]{:S(2)}) async-start(bf16[4,6,24,256]{3,2,1,0:T(8,128)(2,1)} %bitcast.2), calls=%async_computation | async-start | bytes 589824 | tf_op jit(solution)/shard_map/all_to_all | solution.py:437
  9.3 19.7 %collective-permute-start.25 = (bf16[96,728]{1,0:T(8,128)(2,1)S(1)}, bf16[96,728]{1,0:T(8,128)(2,1)S(1)}, u32[]{:S(2)}, u32[]{:S(2)}) collective-permute-start(bf16[96,728]{1,0:T(8,128)(2,1)S(1)} %get-tuple-element.161), channel_id=1, source_target_pairs={{1,0},{2,1},{3,2},{4,3},{5,4},{6,5},{7,6},{8,7},{9,8},{10,9},{11,1... | collective-permute-start | bytes 419336 | tf_op jit(solution)/shard_map/ppermute | solution.py:44
  15.0 14.0 %collective-permute-start.24 = (bf16[96,728]{1,0:T(8,128)(2,1)S(1)}, bf16[96,728]{1,0:T(8,128)(2,1)S(1)}, u32[]{:S(2)}, u32[]{:S(2)}) collective-permute-start(bf16[96,728]{1,0:T(8,128)(2,1)S(1)} %get-tuple-element.162), channel_id=1, source_target_pairs={{0,1},{1,2},{2,3},{3,4},{4,5},{5,6},{6,7},{7,8},{8,9},{9,10},{10,1... | collective-permute-start | bytes 419336 | tf_op jit(solution)/shard_map/ppermute | solution.py:44
  29.0 0.6 copy-start.9
  29.0 0.7 copy-start.10
  29.7 18.1 %copy-start.12 = (s32[2,2]{1,0:T(2,128)S(1)}, s32[2,2]{1,0:T(2,128)}, u32[]{:S(2)}) copy-start(s32[2,2]{1,0:T(2,128)} %sc_ref.8) | copy-start | bytes 52
  29.7 34.3 %copy-start.11 = (f32[2,9,256]{2,0,1:T(2,128)S(1)}, f32[2,9,256]{2,0,1:T(2,128)}, u32[]{:S(2)}) copy-start(f32[2,9,256]{2,0,1:T(2,128)} %param.35) | copy-start | bytes 55300
  41.1 9.5 %collective-permute-start.26 = (bf16[6,96,256]{2,1,0:T(8,128)(2,1)}, bf16[6,96,256]{2,1,0:T(8,128)(2,1)S(1)}, u32[]{:S(2)}, u32[]{:S(2)}) collective-permute-start(bf16[6,96,256]{2,1,0:T(8,128)(2,1)} %get-tuple-element.127.above_ref), channel_id=1, source_target_pairs={{0,1},{1,2},{2,3},{3,4},{4,5},{5,6},{6,7},{7,8},{8,9},{9,10},{10,1... | collective-permute-start | bytes 884744 | tf_op jit(solution)/shard_map/ppermute | solution.py:44
  43.0 12.0 %collective-permute-start.27 = (bf16[6,96,256]{2,1,0:T(8,128)(2,1)}, bf16[6,96,256]{2,1,0:T(8,128)(2,1)S(1)}, u32[]{:S(2)}, u32[]{:S(2)}) collective-permute-start(bf16[6,96,256]{2,1,0:T(8,128)(2,1)} %get-tuple-element.128.below_ref), channel_id=1, source_target_pairs={{1,0},{2,1},{3,2},{4,3},{5,4},{6,5},{7,6},{8,7},{9,8},{10,9},{11,1... | collective-permute-start | bytes 884744 | tf_op jit(solution)/shard_map/ppermute | solution.py:44
  50.5 4.5 %copy-start.3 = (bf16[6,96,256]{2,1,0:T(8,128)(2,1)}, bf16[6,96,256]{2,1,0:T(8,128)(2,1)S(1)}, u32[]{:S(2)}) copy-start(bf16[6,96,256]{2,1,0:T(8,128)(2,1)S(1)} %collective-permute-done.26.up_ref) | copy-start | bytes 884740
  55.0 0.7 copy-start.4
  58.5 6.7 %collective-permute-start.29 = (bf16[1,3,96,256]{3,2,1,0:T(8,128)(2,1)}, bf16[1,3,96,256]{3,2,1,0:T(8,128)(2,1)S(1)}, u32[]{:S(2)}, u32[]{:S(2)}) collective-permute-start(bf16[1,3,96,256]{3,2,1,0:T(8,128)(2,1)} %bitcast.32), channel_id=1, source_target_pairs={{0,63},{1,0},{2,1},{3,2},{4,3},{5,4},{6,5},{7,6},{8,7},{9,8},{10,9... | collective-permute-start | bytes 442376 | tf_op jit(solution)/shard_map/ppermute | solution.py:44
  62.1 6.0 %collective-permute-start.28 = (bf16[1,3,96,256]{3,2,1,0:T(8,128)(2,1)}, bf16[1,3,96,256]{3,2,1,0:T(8,128)(2,1)S(1)}, u32[]{:S(2)}, u32[]{:S(2)}) collective-permute-start(bf16[1,3,96,256]{3,2,1,0:T(8,128)(2,1)} %bitcast.31), channel_id=1, source_target_pairs={{0,1},{1,2},{2,3},{3,4},{4,5},{5,6},{6,7},{7,8},{8,9},{9,10},{10,1... | collective-permute-start | bytes 442376 | tf_op jit(solution)/shard_map/ppermute | solution.py:44
  65.2 2.9 %copy-start.7 = (bf16[1,3,96,256]{3,2,1,0:T(8,128)(2,1)}, bf16[1,3,96,256]{3,2,1,0:T(8,128)(2,1)S(1)}, u32[]{:S(2)}) copy-start(bf16[1,3,96,256]{3,2,1,0:T(8,128)(2,1)S(1)} %collective-permute-done.29.dn_ref) | copy-start | bytes 442372
  68.1 0.7 copy-start.8
  70.4 8.5 %collective-permute-start.6 = (bf16[6,96,256]{2,1,0:T(8,128)(2,1)S(1)}, bf16[6,96,256]{2,1,0:T(8,128)(2,1)S(1)}, u32[]{:S(2)}, u32[]{:S(2)}) collective-permute-start(bf16[6,96,256]{2,1,0:T(8,128)(2,1)S(1)} %get-tuple-element.70), channel_id=1, source_target_pairs={{0,63},{1,0},{2,1},{3,2},{4,3},{5,4},{6,5},{7,6},{8,7},{9,8},{10,9... | collective-permute-start | bytes 884744 | tf_op jit(solution)/shard_map/cond/branch_1_fun/ppermute | solution.py:44
  71.2 10.5 %collective-permute-start.7 = (bf16[6,96,256]{2,1,0:T(8,128)(2,1)S(1)}, bf16[6,96,256]{2,1,0:T(8,128)(2,1)S(1)}, u32[]{:S(2)}, u32[]{:S(2)}) collective-permute-start(bf16[6,96,256]{2,1,0:T(8,128)(2,1)S(1)} %get-tuple-element.71), channel_id=1, source_target_pairs={{0,1},{1,2},{2,3},{3,4},{4,5},{5,6},{6,7},{7,8},{8,9},{9,10},{10,1... | collective-permute-start | bytes 884744 | tf_op jit(solution)/shard_map/cond/branch_1_fun/ppermute | solution.py:44
  88.2 10.7 %collective-permute-start.30 = (bf16[2,3,96,256]{3,2,1,0:T(8,128)(2,1)}, bf16[2,3,96,256]{3,2,1,0:T(8,128)(2,1)S(1)}, u32[]{:S(2)}, u32[]{:S(2)}) collective-permute-start(bf16[2,3,96,256]{3,2,1,0:T(8,128)(2,1)} %get-tuple-element.142), channel_id=1, source_target_pairs={{0,1},{1,2},{2,3},{3,4},{4,5},{5,6},{6,7},{7,8},{8,9},{9,10},{10,1... | collective-permute-start | bytes 884744 | tf_op jit(solution)/shard_map/ppermute | solution.py:44
  88.3 10.7 %collective-permute-start.31 = (bf16[2,3,96,256]{3,2,1,0:T(8,128)(2,1)}, bf16[2,3,96,256]{3,2,1,0:T(8,128)(2,1)S(1)}, u32[]{:S(2)}, u32[]{:S(2)}) collective-permute-start(bf16[2,3,96,256]{3,2,1,0:T(8,128)(2,1)} %get-tuple-element.143), channel_id=1, source_target_pairs={{0,63},{1,0},{2,1},{3,2},{4,3},{5,4},{6,5},{7,6},{8,7},{9,8},{10,9... | collective-permute-start | bytes 884744 | tf_op jit(solution)/shard_map/ppermute | solution.py:44
  99.0 0.7 copy-start.5
  99.0 0.8 copy-start.6
  101.4 7.6 %collective-permute-start.18 = (bf16[6,96,256]{2,1,0:T(8,128)(2,1)S(1)}, bf16[6,96,256]{2,1,0:T(8,128)(2,1)S(1)}, u32[]{:S(2)}, u32[]{:S(2)}) collective-permute-start(bf16[6,96,256]{2,1,0:T(8,128)(2,1)S(1)} %get-tuple-element.82), channel_id=1, source_target_pairs={{0,63},{1,0},{2,1},{3,2},{4,3},{5,4},{6,5},{7,6},{8,7},{9,8},{10,9... | collective-permute-start | bytes 884744 | tf_op jit(solution)/shard_map/cond/branch_1_fun/ppermute | solution.py:44
  103.3 7.4 %collective-permute-start.19 = (bf16[6,96,256]{2,1,0:T(8,128)(2,1)S(1)}, bf16[6,96,256]{2,1,0:T(8,128)(2,1)S(1)}, u32[]{:S(2)}, u32[]{:S(2)}) collective-permute-start(bf16[6,96,256]{2,1,0:T(8,128)(2,1)S(1)} %get-tuple-element.83), channel_id=1, source_target_pairs={{0,1},{1,2},{2,3},{3,4},{4,5},{5,6},{6,7},{7,8},{8,9},{9,10},{10,1... | collective-permute-start | bytes 884744 | tf_op jit(solution)/shard_map/cond/branch_1_fun/ppermute | solution.py:44
  115.1 7.9 %collective-permute-start.33 = (bf16[6,96,256]{2,1,0:T(8,128)(2,1)}, bf16[6,96,256]{2,1,0:T(8,128)(2,1)S(1)}, u32[]{:S(2)}, u32[]{:S(2)}) collective-permute-start(bf16[6,96,256]{2,1,0:T(8,128)(2,1)} %gate.1.own_ref), channel_id=1, source_target_pairs={{1,0},{2,1},{3,2},{4,3},{5,4},{6,5},{7,6},{8,7},{9,8},{10,9},{11,1... | collective-permute-start | bytes 884744 | tf_op jit(solution)/shard_map/ppermute | solution.py:44
  118.1 9.5 %collective-permute-start.32 = (bf16[6,96,256]{2,1,0:T(8,128)(2,1)}, bf16[6,96,256]{2,1,0:T(8,128)(2,1)S(1)}, u32[]{:S(2)}, u32[]{:S(2)}) collective-permute-start(bf16[6,96,256]{2,1,0:T(8,128)(2,1)} %gate.1.own_ref), channel_id=1, source_target_pairs={{0,1},{1,2},{2,3},{3,4},{4,5},{5,6},{6,7},{7,8},{8,9},{9,10},{10,1... | collective-permute-start | bytes 884744 | tf_op jit(solution)/shard_map/ppermute | solution.py:44
  123.0 4.5 %copy-start.1 = (bf16[6,96,256]{2,1,0:T(8,128)(2,1)}, bf16[6,96,256]{2,1,0:T(8,128)(2,1)S(1)}, u32[]{:S(2)}) copy-start(bf16[6,96,256]{2,1,0:T(8,128)(2,1)S(1)} %collective-permute-done.33.dn_ref) | copy-start | bytes 884740
  127.5 0.7 copy-start.2
  138.2 5.4 %collective-permute-start.34 = (bf16[2,768,256]{2,1,0:T(8,128)(2,1)}, bf16[2,768,256]{2,1,0:T(8,128)(2,1)S(1)}, u32[]{:S(2)}, u32[]{:S(2)}) collective-permute-start(bf16[2,768,256]{2,1,0:T(8,128)(2,1)} %get-tuple-element.157), channel_id=1, source_target_pairs={{0,4},{4,0},{1,5},{5,1},{2,6},{6,2},{3,7},{7,3},{8,12},{12,8},{9,1... | collective-permute-start | bytes 2359304 | tf_op jit(solution)/shard_map/ppermute | solution.py:410
  189.1 5.0 %collective-permute-start.35 = (bf16[2,768,256]{2,1,0:T(8,128)(2,1)S(1)}, bf16[2,768,256]{2,1,0:T(8,128)(2,1)S(1)}, u32[]{:S(2)}, u32[]{:S(2)}) collective-permute-start(bf16[2,768,256]{2,1,0:T(8,128)(2,1)S(1)} %bitcast.25), channel_id=1, source_target_pairs={{0,4},{4,0},{1,5},{5,1},{2,6},{6,2},{3,7},{7,3},{8,12},{12,8},{9,1... | collective-permute-start | bytes 2359304 | tf_op jit(solution)/shard_map/ppermute | solution.py:418
where the time goes:
time: 199 us; the launch traced here: 197 us
  Pallas kernels  49.1 us (25%)
  waiting for transfers between devices  46.3 us (23%)
  blocking collectives  43.7 us (22%)
  starting transfers between devices  41.8 us (21%)
  local copies, waits for them, and re-layouts  8.64 us (4%)
  other arithmetic  4.66 us (2%)
  between operations  2.12 us (1%)
    all_to_all x2, blocking collectives, swapped(): lax.all_to_all(pieces, CHIPS, split_axis=0, concat_axis=0, tiled=True)  43.7 us
    ppermute x14, waiting for transfers between devices, from_slab(): return lax.ppermute(value, SLABS, pairs)  42.3 us
    ppermute x14, starting transfers between devices, from_slab(): return lax.ppermute(value, SLABS, pairs)  29.6 us
    pallas_call x1, Pallas kernels, front(): pl.pallas_call(front_kernel, in_specs=[SM] + [VM] * 6, out_specs=[VM] * 4...  11.4 us
    pallas_call x1, Pallas kernels, fold_weights(): pl.pallas_call(weights_kernel, in_specs=[VM] * 3, out_specs=VM, out_shape...  11.3 us
    pallas_call x1, Pallas kernels, grads(): pl.pallas_call(grads_kernel, in_specs=[SM] + [VM] * 6, out_specs=[VM] * 2...  9.9 us
    pallas_call x1, Pallas kernels, later(): pl.pallas_call(later_kernel, in_specs=[SM] + [VM] * 9, out_specs=[VM] * 5...  6.49 us
    all_to_all x1, starting transfers between devices, local(): slab = lax.all_to_all(tile, 'z', split_axis=0, concat_axis=0, tiled=True)  5.84 us
  transfers between devices with their start and end apart: 17, of which 13 were waited for; matrix products, arithmetic and copies ran while one was open for 2% of the time, Pallas kernels for 6%

commit v1 on v0

--- a/solution.py
+++ b/solution.py
@@ -5,6 +5,7 @@
 from jax.experimental.pallas import tpu as pltpu
 from jax.sharding import Mesh, PartitionSpec as P
 
+UNROLL = 6
 BF = jnp.bfloat16
 F32 = jnp.float32
 SLABS = ("y", "xl", "core", "z")
@@ -36,17 +37,41 @@
     return jnp.where(c == want, 1.0, 0.0).astype(BF)
 
 
-def from_slab(value, shift, ring=False):
+def from_slab(value, shift):
     count = lax.axis_size(SLABS)
-    pairs = [(i, i - shift) for i in range(count) if 0 <= i - shift < count]
+    return lax.ppermute(value, SLABS, [(i, (i - shift) % count) for i in range(count)])
+
+
+def swap_slabs(value, odd, ring=False):
+    count = lax.axis_size(SLABS)
+    pairs = [(i, i + 1 if i % 2 == odd else i - 1) for i in range(count)]
     if ring:
-        pairs = [(i, (i - shift) % count) for i in range(count)]
-    return lax.ppermute(value, SLABS, pairs)
-
-
-def masked(window_ref, i, row, height):
-    inside = jnp.logical_and(row + i >= 0, row + i < height)
-    return window_ref[i] * jnp.where(inside, 1.0, 0.0).astype(BF)
+        pairs = [(i, j % count) for i, j in pairs]
+    return lax.ppermute(value, SLABS, [(i, j) for i, j in pairs if 0 <= j < count])
+
+
+def is_even():
+    return lax.axis_index(SLABS) % 2 == 0
+
+
+def inside(row, height):
+    return jnp.where(jnp.logical_and(row >= 0, row < height), 1.0, 0.0)
+
+
+def tap_sum(total, move, windows, i, row, step, height, taps, flip):
+    width = total.shape[0]
+    n = total.shape[1]
+    lines = [windows[a][i] for a in range(3)]
+    moved = mm(move, jnp.concatenate(lines, axis=1))
+    low, high = (2, 0) if flip else (0, 2)
+    for a in range(3):
+        here = slice(a * n, (a + 1) * n)
+        keep = inside(row + i + (a - 1) * step, height)
+        w = [taps[3 * a + b : 3 * a + b + 1, :] * keep for b in range(3)]
+        total = total + moved[:width, here] * w[low]
+        total = total + lines[a].astype(F32) * w[1]
+        total = total + moved[width:, here] * w[high]
+    return total
 
 
 def weights_kernel(proj_ref, point_ref, taps_ref, out_ref):
@@ -74,8 +99,8 @@
 
 
 def front_kernel(
-    rate_ref, feat_ref, up_ref, dn_ref, taps_ref, point_ref, m_ref,
-    mid_ref, u0_ref, above_ref, below_ref, act, so, left, right,
+    rate_ref, feat_ref, near_ref, other_ref, taps_ref, point_ref, m_ref,
+    mid_ref, u0_ref, to_near_ref, to_other_ref, act, so, left, right,
 ):
     part, rate = lax.axis_index("xh"), rate_ref[1]
     rows, width, c = feat_ref.shape[1:]
@@ -87,8 +112,10 @@
         v = v.astype(F32)
         return v * sigmoid(v)
 
-    act[0, 8 : width + 8, :] = activate(up_ref[...])
-    act[rows + 1, 8 : width + 8, :] = activate(dn_ref[...])
+    even = is_even()
+    near, other = near_ref[...].astype(F32), other_ref[...].astype(F32)
+    act[0, 8 : width + 8, :] = activate(jnp.where(even, other, near))
+    act[rows + 1, 8 : width + 8, :] = activate(jnp.where(even, near, other))
 
     def fill(i, carry):
         act[i + 1, 8 : width + 8, :] = activate(feat_ref[part, i])
@@ -122,12 +149,22 @@
         right[at, :] = moved[width:]
         return carry
 
-    lax.fori_loop(0, rows, shift, 0)
+    lax.fori_loop(0, rows, shift, 0, unroll=3)
     n = u0_ref.shape[1]
     total = mm(left[...], m_ref[0]) + mm(so[...], m_ref[1]) + mm(right[...], m_ref[2])
-    above_ref[...] = total[:, :n].astype(BF).reshape(rows, width, n)
     u0_ref[...] = total[:, n : 2 * n]
-    below_ref[...] = total[:, 2 * n :].astype(BF).reshape(rows, width, n)
+    above = total[:, :n].astype(BF).reshape(rows, width, n)
+    below = total[:, 2 * n :].astype(BF).reshape(rows, width, n)
+
+    @pl.when(even)
+    def _():
+        to_near_ref[...] = above
+        to_other_ref[...] = below
+
+    @pl.when(jnp.logical_not(even))
+    def _():
+        to_near_ref[...] = below
+        to_other_ref[...] = above
 
 
 def front(rates, features, up, dn, depth_mid, point_mid, folded):
@@ -155,32 +192,38 @@
 
 
 def first_kernel(
-    rate_ref, u0_ref, above_ref, below_ref, up_ref, dn_ref, pre_ref, out_ref, top_ref, end_ref
+    rate_ref, u0_ref, near_ref, other_ref, of_near_ref, of_other_ref,
+    pre_ref, out_ref, to_near_ref, to_other_ref,
 ):
     rate = rate_ref[0]
     rows, width, n = out_ref.shape
     edge = rows // 2
+    even = is_even()
+
+    def pick(even_ref, odd_ref, row):
+        return jnp.where(even, even_ref[row], odd_ref[row])
 
     def one(i, carry):
         at = pl.ds(pl.multiple_of(i * width, width), width)
         high, low = i - rate, i + rate
-        inner = above_ref[jnp.maximum(high, 0)].astype(F32)
-        outer = up_ref[jnp.minimum(high + rows, rows - 1)].astype(F32)
-        total = u0_ref[at, :] + jnp.where(high >= 0, inner, outer)
-        inner = below_ref[jnp.minimum(low, rows - 1)].astype(F32)
-        outer = dn_ref[jnp.maximum(low - rows, 0)].astype(F32)
-        total = total + jnp.where(low < rows, inner, outer)
+        inner = pick(near_ref, other_ref, jnp.maximum(high, 0))
+        outer = pick(of_other_ref, of_near_ref, jnp.minimum(high + rows, rows - 1))
+        total = u0_ref[at, :] + jnp.where(high >= 0, inner, outer).astype(F32)
+        inner = pick(other_ref, near_ref, jnp.minimum(low, rows - 1))
+        outer = pick(of_near_ref, of_other_ref, jnp.maximum(low - rows, 0))
+        total = total + jnp.where(low < rows, inner, outer).astype(F32)
         pre_ref[at, :] = total
         out_ref[i] = (total * sigmoid(total)).astype(BF)
         return carry
 
     lax.fori_loop(0, rows, one, 0)
-    top_ref[...] = out_ref[:edge]
-    end_ref[...] = out_ref[rows - edge :]
-
-
-def first(rates, u0, above, below, up, dn):
-    rows, width, n = above.shape
+    top, end = out_ref[:edge], out_ref[rows - edge :]
+    to_near_ref[...] = jnp.where(even, end, top)
+    to_other_ref[...] = jnp.where(even, top, end)
+
+
+def first(rates, u0, near, other, of_near, of_other):
+    rows, width, n = near.shape
     edge = rows // 2
     return pl.pallas_call(
         first_kernel,
@@ -193,13 +236,14 @@
             jax.ShapeDtypeStruct((edge, width, n), BF),
         ],
         name="first",
-    )(rates, u0, above, below, up, dn)
-
-
-def cut_kernel(sc_ref, up_ref, own_ref, dn_ref, p0_ref, m0_ref, p1_ref, m1_ref):
+    )(rates, u0, near, other, of_near, of_other)
+
+
+def cut_kernel(sc_ref, near_ref, own_ref, other_ref, p0_ref, m0_ref, p1_ref, m1_ref):
     many, rows, width, n = own_ref.shape
     edge = rows // 2
     outs = ((p0_ref, m0_ref), (p1_ref, m1_ref))
+    even = is_even()
 
     def one(i, carry):
         for l in range(2):
@@ -208,17 +252,18 @@
             rest = rate - (rate + edge - 1) // rows * rows
             for sign in (1, -1):
                 j = i + sign * rest
-                near = own_ref[k, jnp.clip(j, 0, rows - 1)]
-                far = dn_ref[k, jnp.clip(j - rows, 0, edge - 1)]
-                back = up_ref[k, jnp.clip(j + edge, 0, edge - 1)]
-                row = jnp.where(j < 0, back, jnp.where(j < rows, near, far))
+                own = own_ref[k, jnp.clip(j, 0, rows - 1)]
+                low = j < 0
+                far = jnp.where(low, j + edge, jnp.clip(j - rows, 0, edge - 1))
+                far = jnp.where(low == even, other_ref[k, far], near_ref[k, far])
+                row = jnp.where(jnp.logical_and(j >= 0, j < rows), own, far)
                 outs[l][(1 - sign) // 2][i] = row
         return carry
 
     lax.fori_loop(0, rows, one, 0)
 
 
-def cut(rates, up, own, dn):
+def cut(rates, near, own, other):
     _, rows, width, n = own.shape
     return pl.pallas_call(
         cut_kernel,
@@ -226,39 +271,38 @@
         out_specs=[VM] * 4,
         out_shape=[jax.ShapeDtypeStruct((rows, width, n), BF)] * 4,
         name="cut",
-    )(rates, up, own, dn)
+    )(rates, near, own, other)
 
 
 def later_kernel(
     sc_ref, own_ref, p0_ref, m0_ref, p1_ref, m1_ref, up_ref, join_ref, taps_ref, point_ref,
-    back_ref, top_ref, end_ref, grad_ref, direct_ref, conv,
+    back_ref, to_near_ref, to_other_ref, grad_ref, direct_ref, conv,
 ):
     rows, width, n = own_ref.shape
     first, height = lax.axis_index(SLABS) * rows, lax.axis_size(SLABS) * rows
     windows = ((m0_ref, own_ref, p0_ref), (m1_ref, own_ref, p1_ref))
+    even = is_even()
     for l in range(2):
         move = shifter(width, sc_ref[l, 1])
 
         def one(i, carry, l=l, move=move):
-            total = jnp.zeros((width, n), F32)
-            for a in range(3):
-                row = masked(windows[l][a], i, first + (a - 1) * sc_ref[l, 0], height)
-                moved = mm(move, row)
-                total = total + moved[:width] * taps_ref[l, 3 * a : 3 * a + 1, :]
-                total = total + row.astype(F32) * taps_ref[l, 3 * a + 1 : 3 * a + 2, :]
-                total = total + moved[width:] * taps_ref[l, 3 * a + 2 : 3 * a + 3, :]
+            total = tap_sum(
+                jnp.zeros((width, n), F32), move, windows[l], i, first, sc_ref[l, 0], height,
+                taps_ref[l], False,
+            )
             conv[pl.ds(pl.multiple_of(i * width, width), width), :] = total.astype(BF)
             return carry
 
-        lax.fori_loop(0, rows, one, 0)
+        lax.fori_loop(0, rows, one, 0, unroll=UNROLL)
         pre = mm(conv[...], point_ref[l])
         block = mm(up_ref[...], join_ref[(l + 1) * n : (l + 2) * n, :], NT)
         gate = (block * slope(pre)).astype(BF)
         back = mm(gate, point_ref[l], NT).astype(BF)
         back = back.reshape(rows, width, n)
         back_ref[l] = back
-        top_ref[l] = back[: rows // 2]
-        end_ref[l] = back[rows - rows // 2 :]
+        top, end = back[: rows // 2], back[rows - rows // 2 :]
+        to_near_ref[l] = jnp.where(even, end, top)
+        to_other_ref[l] = jnp.where(even, top, end)
         grad_ref[l] = mm(conv[...], gate, TN)
     direct_ref[...] = mm(up_ref[...], join_ref[:n, :], NT)
 
@@ -294,16 +338,13 @@
         at = pl.ds(pl.multiple_of(i * width, width), width)
         total = direct_ref[at, :]
         for l in range(2):
-            for a in range(3):
-                row = masked(windows[l][a], i, first - (a - 1) * sc_ref[l, 0], height)
-                moved = mm(moves[l], row)
-                total = total + moved[width:] * taps_ref[l, 3 * a : 3 * a + 1, :]
-                total = total + row.astype(F32) * taps_ref[l, 3 * a + 1 : 3 * a + 2, :]
-                total = total + moved[:width] * taps_ref[l, 3 * a + 2 : 3 * a + 3, :]
+            total = tap_sum(
+                total, moves[l], windows[l], i, first, -sc_ref[l, 0], height, taps_ref[l], True
+            )
         out_ref[i] = (total * slope(pre_ref[at, :])).astype(BF)
         return carry
 
-    lax.fori_loop(0, rows, one, 0)
+    lax.fori_loop(0, rows, one, 0, unroll=2)
 
 
 def gate(rates, back, windows, direct, pre, depth):
@@ -317,12 +358,13 @@
 
 
 def grads_kernel(
-    sc_ref, up_ref, own_ref, dn_ref, mid_ref, m_ref, later_ref, keep_ref, give_ref,
+    sc_ref, near_ref, own_ref, other_ref, mid_ref, m_ref, later_ref, keep_ref, give_ref,
     g0, g1, g2, back,
 ):
     rate_row, rate_col = sc_ref[0], sc_ref[1]
     rows, width, n = own_ref.shape
     c = mid_ref.shape[1]
+    even = is_even()
     move = shifter(width, rate_col)
 
     def one(i, carry):
@@ -331,16 +373,18 @@
             j = i - (a - 1) * rate_row
             row = own_ref[jnp.clip(j, 0, rows - 1)]
             if a == 0:
-                row = jnp.where(j < rows, row, dn_ref[jnp.maximum(j - rows, 0)])
+                far = jnp.maximum(j - rows, 0)
+                row = jnp.where(j < rows, row, jnp.where(even, near_ref[far], other_ref[far]))
             if a == 2:
-                row = jnp.where(j >= 0, row, up_ref[jnp.minimum(j + rows, rows - 1)])
+                far = jnp.minimum(j + rows, rows - 1)
+                row = jnp.where(j >= 0, row, jnp.where(even, other_ref[far], near_ref[far]))
             moved = mm(move, row).astype(BF)
             g0[at, a * n : (a + 1) * n] = moved[width:]
             g1[at, a * n : (a + 1) * n] = row
             g2[at, a * n : (a + 1) * n] = moved[:width]
         return carry
 
-    lax.fori_loop(0, rows, one, 0)
+    lax.fori_loop(0, rows, one, 0, unroll=UNROLL)
     total = mm(g0[...], m_ref[0], NT) + mm(g1[...], m_ref[1], NT) + mm(g2[...], m_ref[2], NT)
     back[...] = total.astype(BF)
     core = lax.axis_index("core")
@@ -348,13 +392,13 @@
     def put(k, lo, hi, wide, value):
         @pl.when(core == k // 2)
         def _():
-            keep_ref[k % 2, lo:hi, :wide] = value
+            keep_ref[k % 2, lo:hi, :wide] = value.astype(BF)
 
         @pl.when(core != k // 2)
         def _():
             give_ref[k % 2, lo:hi, :wide] = value.astype(BF)
 
-    keep_ref[:, c:, :] = jnp.zeros((2, keep_ref.shape[1] - c, n), F32)
+    keep_ref[:, c:, :] = jnp.zeros((2, keep_ref.shape[1] - c, n), BF)
     give_ref[:, c:, :] = jnp.zeros((2, keep_ref.shape[1] - c, n), BF)
     for k in range(3):
         lo, hi = k * n, min((k + 1) * n, c)
@@ -375,7 +419,7 @@
         in_specs=[SM] + [VM] * 6,
         out_specs=[VM] * 2,
         out_shape=[
-            jax.ShapeDtypeStruct((2, 3 * n, n), F32),
+            jax.ShapeDtypeStruct((2, 3 * n, n), BF),
             jax.ShapeDtypeStruct((2, 3 * n, n), BF),
         ],
         scratch_shapes=[pltpu.VMEM((cells, 3 * n), BF)] * 3 + [pltpu.VMEM((cells, c), BF)],
@@ -383,18 +427,18 @@
     )(rates, up, own, dn, mid, folded, later_grads)
 
 
-def row_windows(own, top, end, rates):
+def row_windows(own, near, other, rates):
     rows = own.shape[1]
-    below = from_slab(top, 1, ring=True)
-    above = from_slab(end, -1, ring=True)
-    p0, m0, p1, m1 = cut(rates, above, own, below)
+    near = swap_slabs(near, 0, ring=True)
+    other = swap_slabs(other, 1, ring=True)
+    p0, m0, p1, m1 = cut(rates, near, own, other)
     whole = (rates[:, 0] + rows // 2 - 1) // rows
 
     def at(q):
         def fetch(plus, minus):
             if q == 0:
                 return plus, minus
-            return from_slab(plus, q, ring=True), from_slab(minus, -q, ring=True)
+            return from_slab(plus, q), from_slab(minus, -q)
 
         return fetch
 
@@ -407,7 +451,7 @@
     swap = [(0, 1), (1, 0)]
     half, rows, lanes = keep.shape
     chips = lax.axis_size(CHIPS)
-    mine = (keep + lax.ppermute(give, "core", swap).astype(F32)).astype(BF)
+    mine = (keep.astype(F32) + lax.ppermute(give, "core", swap).astype(F32)).astype(BF)
     mine = mine.reshape(chips, half * rows // chips, lanes)
 
     def swapped(pieces):
@@ -430,28 +474,29 @@
     n = point_later.shape[1]
     cells = rows * width
     groups = lax.axis_size("z")
-    down = from_slab(features[part, 0], 1)
-    up = from_slab(features[part, rows - 1], -1)
+    even = is_even()
+    near = swap_slabs(features[part, jnp.where(even, rows - 1, 0)], 0)
+    other = swap_slabs(features[part, jnp.where(even, 0, rows - 1)], 1)
     folded = fold_weights(projection, point_first, depth_first)
     tile = upstream[part].reshape(groups, rows, width // groups, n)
     slab = lax.all_to_all(tile, "z", split_axis=0, concat_axis=0, tiled=True)
     slab = slab.transpose(1, 0, 2, 3).reshape(cells, n)
 
-    up, down, slab = lax.optimization_barrier((up, down, slab))
-    mid, u0, above, below = front(
-        rate_first, features, up, down, depth_mid, point_mid, folded
+    near, other, slab = lax.optimization_barrier((near, other, slab))
+    mid, u0, near, other = front(
+        rate_first, features, near, other, depth_mid, point_mid, folded
     )
-    from_up = from_slab(above, -1)
-    from_down = from_slab(below, 1)
-    first_pre, first_out, top, end = first(rate_first, u0, above, below, from_up, from_down)
-    windows = row_windows(first_out[None], top[None], end[None], rates_later)
-    back, top, end, later_grads, direct = later(
+    first_pre, first_out, near, other = first(
+        rate_first, u0, near, other, swap_slabs(near, 0), swap_slabs(other, 1)
+    )
+    windows = row_windows(first_out[None], near[None], other[None], rates_later)
+    back, near, other, later_grads, direct = later(
         rates_later, first_out, windows, slab, joining, depth_later, point_later
     )
-    windows = row_windows(back, top, end, rates_later)
+    windows = row_windows(back, near, other, rates_later)
     gated = gate(rates_later, back, windows, direct, first_pre, depth_later)
     keep, give = grads(
-        rate_first, from_slab(gated, -1), gated, from_slab(gated, 1), mid, folded, later_grads
+        rate_first, swap_slabs(gated, 0), gated, swap_slabs(gated, 1), mid, folded, later_grads
     )
     total = total_over_devices(keep, give).astype(F32)
     grad_mid = jnp.concatenate([total[0], total[1], total[2]], axis=1)[:c, :c]

time: 199 us -> 216 us (1.085)
  waiting for transfers between devices: 46.3 us -> 69.3 us
  Pallas kernels: 49.1 us -> 45.5 us
  starting transfers between devices: 41.8 us -> 44 us
    ppermute x15 -> x19, waiting for transfers between devices: 44.4 us -> 67.4 us  [the longest x8 40.1 us: from_slab(): lax.ppermute(value, SLABS, [(i, (i - shift) % count) for i in range(count)])]
    ppermute x15 -> x19, starting transfers between devices: 32.8 us -> 37.5 us  [the longest x10 22.8 us: swap_slabs(): lax.ppermute(value, SLABS, [(i, j) for i, j in pairs if 0 <= j < count])]
    all_to_all x1, starting transfers between devices: 5.84 us -> 3.45 us  [local(): slab = lax.all_to_all(tile, 'z', split_axis=0, concat_axis=0, tiled=True)]
  transfers between devices with their start and end apart: 17 -> 21, of which waited for: 13 -> 16; matrix products, arithmetic and copies ran while one was open for 2% -> 1% of each run, Pallas kernels for 6% -> 5%
where the time goes in v1:
time: 216 us; the launch traced here: 215 us
  waiting for transfers between devices  69.3 us (32%)
  Pallas kernels  45.5 us (21%)
  starting transfers between devices  44 us (20%)
  blocking collectives  41.9 us (19%)
  local copies, waits for them, and re-layouts  7.73 us (4%)
  other arithmetic  4.36 us (2%)
    all_to_all x2, blocking collectives, swapped(): lax.all_to_all(pieces, CHIPS, split_axis=0, concat_axis=0, tiled=True)  41.9 us
    ppermute x8, waiting for transfers between devices, from_slab(): lax.ppermute(value, SLABS, [(i, (i - shift) % count) for i in range(count)])  40.1 us
    ppermute x10, waiting for transfers between devices, swap_slabs(): lax.ppermute(value, SLABS, [(i, j) for i, j in pairs if 0 <= j < count])  24.8 us
    ppermute x10, starting transfers between devices, swap_slabs(): lax.ppermute(value, SLABS, [(i, j) for i, j in pairs if 0 <= j < count])  22.8 us
    ppermute x8, starting transfers between devices, from_slab(): lax.ppermute(value, SLABS, [(i, (i - shift) % count) for i in range(count)])  14.7 us
    pallas_call x1, Pallas kernels, fold_weights(): pl.pallas_call(weights_kernel, in_specs=[VM] * 3, out_specs=VM, out_shape...  11.3 us
    pallas_call x1, Pallas kernels, front(): pl.pallas_call(front_kernel, in_specs=[SM] + [VM] * 6, out_specs=[VM] * 4...  11.2 us
    pallas_call x1, Pallas kernels, grads(): pl.pallas_call(grads_kernel, in_specs=[SM] + [VM] * 6, out_specs=[VM] * 2...  8.79 us
  transfers between devices with their start and end apart: 21, of which 16 were waited for; matrix products, arithmetic and copies ran while one was open for 1% of the time, Pallas kernels for 5%

profile of v1, /device:TPU:1, one launch (start us, length us, event | category | flops | bytes accessed | tf_op | source)
XLA Modules:
  0.0 215.4 jit_solution(1220759901477592719)
XLA Ops:
  1.7 7.0 %collective-permute-start.25 = (bf16[96,728]{1,0:T(8,128)(2,1)S(1)}, bf16[96,728]{1,0:T(8,128)(2,1)S(1)}, u32[]{:S(2)}, u32[]{:S(2)}) collective-permute-start(bf16[96,728]{1,0:T(8,128)(2,1)S(1)} %get-tuple-element.161), channel_id=1, source_target_pairs={{1,2},{2,1},{3,4},{4,3},{5,6},{6,5},{7,8},{8,7},{9,10},{10,9},{11,... | collective-permute-start | bytes 419336 | tf_op jit(solution)/shard_map/ppermute | solution.py:50
  9.6 3.5 %all-to-all-start = ((bf16[4,6,24,256]{3,2,1,0:T(8,128)(2,1)}), bf16[4,6,24,256]{3,2,1,0:T(8,128)(2,1)S(1)}, u32[]{:S(2)}, u32[]{:S(2)}) async-start(bf16[4,6,24,256]{3,2,1,0:T(8,128)(2,1)} %bitcast.2), calls=%async_computation | async-start | bytes 589824 | tf_op jit(solution)/shard_map/all_to_all | solution.py:482
  13.1 11.3 %fold_weights.1.m_ref = bf16[3,728,768]{2,1,0:T(8,128)(2,1)} custom-call(bf16[728,2048]{1,0:T(8,128)(2,1)} %proj_ref.1, bf16[2048,256]{1,0:T(8,128)(2,1)} %point_ref.3, f32[9,2048]{1,0:T(8,128)} %taps_ref.4), custom_call_target="tpu_custom_call" | custom-call | flops 6870269952 | bytes 11927552 | tf_op jit(solution)/shard_map/fold_weights/pallas_call | solution.py:89
  25.9 11.2 %front.1 = (bf16[576,728]{1,0:T(8,128)(2,1)}, f32[576,256]{1,0:T(8,128)}, bf16[6,96,256]{2,1,0:T(8,128)(2,1)}, bf16[6,96,256]{2,1,0:T(8,128)(2,1)}) custom-call(s32[2]{0:T(128)} %sc_ref.9, bf16[2,6,96,728]{3,2,1,0:T(8,128)(2,1)} %feat_ref.1, bf16[96,728]{1,0:T(8,128)(2,1)} %copy-done.10, bf16[96,728]{1,0:T(8,128)(2,1)} %copy-done.9, f32[9,728]{1,0:T(8,128)} %taps_ref.5, ...), custom_call_target="tpu_custom_call" | custom-call | tf_op jit(solution)/shard_map/front/pallas_call | solution.py:174
  38.5 4.3 %collective-permute-start.27 = (bf16[6,96,256]{2,1,0:T(8,128)(2,1)}, bf16[6,96,256]{2,1,0:T(8,128)(2,1)S(1)}, u32[]{:S(2)}, u32[]{:S(2)}) collective-permute-start(bf16[6,96,256]{2,1,0:T(8,128)(2,1)} %get-tuple-element.128.other_ref), channel_id=1, source_target_pairs={{1,2},{2,1},{3,4},{4,3},{5,6},{6,5},{7,8},{8,7},{9,10},{10,9},{11,... | collective-permute-start | bytes 884744 | tf_op jit(solution)/shard_map/ppermute | solution.py:50
  43.1 2.6 %collective-permute-done.26.of_near_ref = bf16[6,96,256]{2,1,0:T(8,128)(2,1)S(1)} collective-permute-done((bf16[6,96,256]{2,1,0:T(8,128)(2,1)}, bf16[6,96,256]{2,1,0:T(8,128)(2,1)S(1)}, u32[]{:S(2)}, u32[]{:S(2)}) %collective-permute-start.26) | collective-permute-done | bytes 294944 | tf_op jit(solution)/shard_map/ppermute | solution.py:50
  45.7 4.2 %collective-permute-done.27.of_other_ref = bf16[6,96,256]{2,1,0:T(8,128)(2,1)S(1)} collective-permute-done((bf16[6,96,256]{2,1,0:T(8,128)(2,1)}, bf16[6,96,256]{2,1,0:T(8,128)(2,1)S(1)}, u32[]{:S(2)}, u32[]{:S(2)}) %collective-permute-start.27) | collective-permute-done | bytes 294944 | tf_op jit(solution)/shard_map/ppermute | solution.py:50
  50.7 2.8 %first.1 = (f32[576,256]{1,0:T(8,128)}, bf16[6,96,256]{2,1,0:T(8,128)(2,1)}, bf16[3,96,256]{2,1,0:T(8,128)(2,1)}, bf16[3,96,256]{2,1,0:T(8,128)(2,1)}) custom-call(s32[2]{0:T(128)} %sc_ref.9, f32[576,256]{1,0:T(8,128)} %get-tuple-element.126.u0_ref, bf16[6,96,256]{2,1,0:T(8,128)(2,1)} %get-tuple-element.127.near_ref, ...), custom_call_target="tpu_custom_call" | custom-call | tf_op jit(solution)/shard_map/first/pallas_call | solution.py:228
  53.5 3.6 %collective-permute-start.29 = (bf16[1,3,96,256]{3,2,1,0:T(8,128)(2,1)}, bf16[1,3,96,256]{3,2,1,0:T(8,128)(2,1)S(1)}, u32[]{:S(2)}, u32[]{:S(2)}) collective-permute-start(bf16[1,3,96,256]{3,2,1,0:T(8,128)(2,1)} %bitcast.32), channel_id=1, source_target_pairs={{0,63},{1,2},{2,1},{3,4},{4,3},{5,6},{6,5},{7,8},{8,7},{9,10},{10,... | collective-permute-start | bytes 442376 | tf_op jit(solution)/shard_map/ppermute | solution.py:50
  63.8 10.4 %conditional.4 = ((bf16[6,96,256]{2,1,0:T(8,128)(2,1)S(1)}, bf16[6,96,256]{2,1,0:T(8,128)(2,1)S(1)})) conditional(s32[]{:T(128)} %bitcast.5, (bf16[6,96,256]{2,1,0:T(8,128)(2,1)S(1)}, bf16[6,96,256]{2,1,0:T(8,128)(2,1)S(1)}) %tuple.70, (bf16[6,96,256]{2,1,0:T(8,128)(2,1)S(1)}, ...), branch_computations={%region_0.1_spmd, %region_1.2_spmd, %region_2.3_spmd, %region_3.4_... | conditional | bytes 3539048 | solution.py:446
  66.6 7.5 %collective-permute-done.4 = bf16[6,96,256]{2,1,0:T(8,128)(2,1)S(1)} collective-permute-done((bf16[6,96,256]{2,1,0:T(8,128)(2,1)S(1)}, bf16[6,96,256]{2,1,0:T(8,128)(2,1)S(1)}, u32[]{:S(2)}, u32[]{:S(2)}) %collective-permute-start.4) | collective-permute-done | bytes 294944 | tf_op jit(solution)/shard_map/cond/branch_3_fun/ppermute | solution.py:42
  74.2 16.7 %conditional.5 = ((bf16[6,96,256]{2,1,0:T(8,128)(2,1)S(1)}, bf16[6,96,256]{2,1,0:T(8,128)(2,1)S(1)})) conditional(s32[]{:T(128)} %bitcast.9, (bf16[6,96,256]{2,1,0:T(8,128)(2,1)S(1)}, bf16[6,96,256]{2,1,0:T(8,128)(2,1)S(1)}) %tuple.71, (bf16[6,96,256]{2,1,0:T(8,128)(2,1)S(1)}, ...), branch_computations={%region_4.5_spmd, %region_5.6_spmd, %region_6.7_spmd, %region_7.8_... | conditional | bytes 3539048 | solution.py:446
  74.3 3.0 %collective-permute-start.8 = (bf16[6,96,256]{2,1,0:T(8,128)(2,1)S(1)}, bf16[6,96,256]{2,1,0:T(8,128)(2,1)S(1)}, u32[]{:S(2)}, u32[]{:S(2)}) collective-permute-start(bf16[6,96,256]{2,1,0:T(8,128)(2,1)S(1)} %get-tuple-element.72), channel_id=1, source_target_pairs={{0,62},{1,63},{2,0},{3,1},{4,2},{5,3},{6,4},{7,5},{8,6},{9,7},{10,... | collective-permute-start | bytes 884744 | tf_op jit(solution)/shard_map/cond/branch_2_fun/ppermute | solution.py:42
  77.3 7.4 %collective-permute-done.8 = bf16[6,96,256]{2,1,0:T(8,128)(2,1)S(1)} collective-permute-done((bf16[6,96,256]{2,1,0:T(8,128)(2,1)S(1)}, bf16[6,96,256]{2,1,0:T(8,128)(2,1)S(1)}, u32[]{:S(2)}, u32[]{:S(2)}) %collective-permute-start.8) | collective-permute-done | bytes 294944 | tf_op jit(solution)/shard_map/cond/branch_2_fun/ppermute | solution.py:42
  84.8 6.1 %collective-permute-done.9 = bf16[6,96,256]{2,1,0:T(8,128)(2,1)S(1)} collective-permute-done((bf16[6,96,256]{2,1,0:T(8,128)(2,1)S(1)}, bf16[6,96,256]{2,1,0:T(8,128)(2,1)S(1)}, u32[]{:S(2)}, u32[]{:S(2)}) %collective-permute-start.9) | collective-permute-done | bytes 294944 | tf_op jit(solution)/shard_map/cond/branch_2_fun/ppermute | solution.py:42
  90.9 4.6 %later.1 = (bf16[2,6,96,256]{3,2,1,0:T(8,128)(2,1)}, bf16[2,3,96,256]{3,2,1,0:T(8,128)(2,1)}, bf16[2,3,96,256]{3,2,1,0:T(8,128)(2,1)}, f32[2,256,256]{2,1,0:T(8,128)}, f32[576,256]{1,0:T(8,128)}) custom-call(s32[2,2]{1,0:T(2,128)} %sc_ref.8, bf16[6,96,256]{2,1,0:T(8,128)(2,1)} %get-tuple-element.129.own_ref, ...), custom_call_target="tpu_custom_call" | custom-call | tf_op jit(solution)/shard_map/later/pallas_call | solution.py:313
  96.9 7.8 %collective-permute-done.30.near_ref = bf16[2,3,96,256]{3,2,1,0:T(8,128)(2,1)S(1)} collective-permute-done((bf16[2,3,96,256]{3,2,1,0:T(8,128)(2,1)}, bf16[2,3,96,256]{3,2,1,0:T(8,128)(2,1)S(1)}, u32[]{:S(2)}, u32[]{:S(2)}) %collective-permute-start.30) | collective-permute-done | bytes 294944 | tf_op jit(solution)/shard_map/ppermute | solution.py:50
  108.7 10.1 %conditional.6 = ((bf16[6,96,256]{2,1,0:T(8,128)(2,1)S(1)}, bf16[6,96,256]{2,1,0:T(8,128)(2,1)S(1)})) conditional(s32[]{:T(128)} %bitcast.5, (bf16[6,96,256]{2,1,0:T(8,128)(2,1)S(1)}, bf16[6,96,256]{2,1,0:T(8,128)(2,1)S(1)}) %tuple.72, (bf16[6,96,256]{2,1,0:T(8,128)(2,1)S(1)}, ...), branch_computations={%region_8.9_spmd, %region_9.10_spmd, %region_10.11_spmd, %region_1... | conditional | bytes 3539048 | solution.py:446
  108.9 2.7 %collective-permute-start.17 = (bf16[6,96,256]{2,1,0:T(8,128)(2,1)S(1)}, bf16[6,96,256]{2,1,0:T(8,128)(2,1)S(1)}, u32[]{:S(2)}, u32[]{:S(2)}) collective-permute-start(bf16[6,96,256]{2,1,0:T(8,128)(2,1)S(1)} %get-tuple-element.81), channel_id=1, source_target_pairs={{0,3},{1,4},{2,5},{3,6},{4,7},{5,8},{6,9},{7,10},{8,11},{9,12},{10... | collective-permute-start | bytes 884744 | tf_op jit(solution)/shard_map/cond/branch_3_fun/ppermute | solution.py:42
  111.5 7.2 %collective-permute-done.16 = bf16[6,96,256]{2,1,0:T(8,128)(2,1)S(1)} collective-permute-done((bf16[6,96,256]{2,1,0:T(8,128)(2,1)S(1)}, bf16[6,96,256]{2,1,0:T(8,128)(2,1)S(1)}, u32[]{:S(2)}, u32[]{:S(2)}) %collective-permute-start.16) | collective-permute-done | bytes 294944 | tf_op jit(solution)/shard_map/cond/branch_3_fun/ppermute | solution.py:42
  118.9 18.1 %conditional.7 = ((bf16[6,96,256]{2,1,0:T(8,128)(2,1)S(1)}, bf16[6,96,256]{2,1,0:T(8,128)(2,1)S(1)})) conditional(s32[]{:T(128)} %bitcast.9, (bf16[6,96,256]{2,1,0:T(8,128)(2,1)S(1)}, bf16[6,96,256]{2,1,0:T(8,128)(2,1)S(1)}) %tuple.73, (bf16[6,96,256]{2,1,0:T(8,128)(2,1)S(1)}, ...), branch_computations={%region_12.13_spmd, %region_13.14_spmd, %region_14.15_spmd, %regio... | conditional | bytes 3539048 | solution.py:446
  119.1 6.1 %collective-permute-start.20 = (bf16[6,96,256]{2,1,0:T(8,128)(2,1)S(1)}, bf16[6,96,256]{2,1,0:T(8,128)(2,1)S(1)}, u32[]{:S(2)}, u32[]{:S(2)}) collective-permute-start(bf16[6,96,256]{2,1,0:T(8,128)(2,1)S(1)} %get-tuple-element.84), channel_id=1, source_target_pairs={{0,62},{1,63},{2,0},{3,1},{4,2},{5,3},{6,4},{7,5},{8,6},{9,7},{10,... | collective-permute-start | bytes 884744 | tf_op jit(solution)/shard_map/cond/branch_2_fun/ppermute | solution.py:42
  125.2 5.3 %collective-permute-done.20 = bf16[6,96,256]{2,1,0:T(8,128)(2,1)S(1)} collective-permute-done((bf16[6,96,256]{2,1,0:T(8,128)(2,1)S(1)}, bf16[6,96,256]{2,1,0:T(8,128)(2,1)S(1)}, u32[]{:S(2)}, u32[]{:S(2)}) %collective-permute-start.20) | collective-permute-done | bytes 294944 | tf_op jit(solution)/shard_map/cond/branch_2_fun/ppermute | solution.py:42
  130.5 6.4 %collective-permute-done.21 = bf16[6,96,256]{2,1,0:T(8,128)(2,1)S(1)} collective-permute-done((bf16[6,96,256]{2,1,0:T(8,128)(2,1)S(1)}, bf16[6,96,256]{2,1,0:T(8,128)(2,1)S(1)}, u32[]{:S(2)}, u32[]{:S(2)}) %collective-permute-start.21) | collective-permute-done | bytes 294944 | tf_op jit(solution)/shard_map/cond/branch_2_fun/ppermute | solution.py:42
  137.0 3.7 %gate.1.own_ref = bf16[6,96,256]{2,1,0:T(8,128)(2,1)} custom-call(s32[2,2]{1,0:T(2,128)} %sc_ref.8, bf16[2,6,96,256]{3,2,1,0:T(8,128)(2,1)} %get-tuple-element.141.own_ref, bf16[6,96,256]{2,1,0:T(8,128)(2,1)S(1)} %get-tuple-element.146.p0_ref, bf16[6,96,256]{2,1,0:T(8,128)(2,1)S(1)} %get-tuple-element.147.m0_ref, ...), custom_call_target="tpu_custom_call" | custom-call | tf_op jit(solution)/shard_map/gate/pallas_call | solution.py:351
  140.7 4.2 %collective-permute-start.33 = (bf16[6,96,256]{2,1,0:T(8,128)(2,1)}, bf16[6,96,256]{2,1,0:T(8,128)(2,1)S(1)}, u32[]{:S(2)}, u32[]{:S(2)}) collective-permute-start(bf16[6,96,256]{2,1,0:T(8,128)(2,1)} %gate.1.own_ref), channel_id=1, source_target_pairs={{1,2},{2,1},{3,4},{4,3},{5,6},{6,5},{7,8},{8,7},{9,10},{10,9},{11,... | collective-permute-start | bytes 884744 | tf_op jit(solution)/shard_map/ppermute | solution.py:50
  145.7 6.3 %collective-permute-done.33.other_ref = bf16[6,96,256]{2,1,0:T(8,128)(2,1)S(1)} collective-permute-done((bf16[6,96,256]{2,1,0:T(8,128)(2,1)}, bf16[6,96,256]{2,1,0:T(8,128)(2,1)S(1)}, u32[]{:S(2)}, u32[]{:S(2)}) %collective-permute-start.33) | collective-permute-done | bytes 294944 | tf_op jit(solution)/shard_map/ppermute | solution.py:50
  152.8 8.8 %grads.1 = (bf16[2,768,256]{2,1,0:T(8,128)(2,1)}, bf16[2,768,256]{2,1,0:T(8,128)(2,1)}) custom-call(s32[2]{0:T(128)} %sc_ref.9, bf16[6,96,256]{2,1,0:T(8,128)(2,1)} %copy-done.2, bf16[6,96,256]{2,1,0:T(8,128)(2,1)} %gate.1.own_ref, bf16[6,96,256]{2,1,0:T(8,128)(2,1)} %copy-done.1, bf16[576,728]{1,0:T(8,128)(2,1)} %get-tuple-element.154.mid_ref, ...), custom_call_target="tpu_custom_call" | custom-call | tf_op jit(solution)/shard_map/grads/pallas_call | solution.py:417
  161.6 2.5 %collective-permute-done.34 = bf16[2,768,256]{2,1,0:T(8,128)(2,1)S(1)} collective-permute-done((bf16[2,768,256]{2,1,0:T(8,128)(2,1)}, bf16[2,768,256]{2,1,0:T(8,128)(2,1)S(1)}, u32[]{:S(2)}, u32[]{:S(2)}) %collective-permute-start.34) | collective-permute-done | bytes 786464 | tf_op jit(solution)/shard_map/ppermute | solution.py:454
  165.4 23.4 %all_to_all.15 = bf16[64,24,256]{2,1,0:T(8,128)(2,1)S(1)} all-to-all(bf16[64,24,256]{2,1,0:T(8,128)(2,1)S(1)} %bitcast.24), channel_id=1, replica_groups=mesh['xh'=2,'y'=4,'xl'=2,'core'=2,'z'=4] {'xh','y','xl','z'}, dimensions={0} | all-to-all | bytes 1572864 | tf_op jit(solution)/shard_map/all_to_all | solution.py:458
  189.0 18.5 %all_to_all.16 = bf16[64,24,256]{2,1,0:T(8,128)(2,1)S(1)} all-to-all(bf16[64,24,256]{2,1,0:T(8,128)(2,1)S(1)} %broadcast_in_dim.18), channel_id=1, replica_groups=mesh['xh'=2,'y'=4,'xl'=2,'core'=2,'z'=4] {'xh','y','xl','z'}, dimensions={0} | all-to-all | bytes 1572864 | tf_op jit(solution)/shard_map/all_to_all | solution.py:458
  207.5 3.1 %collective-permute-start.35 = (bf16[2,768,256]{2,1,0:T(8,128)(2,1)S(1)}, bf16[2,768,256]{2,1,0:T(8,128)(2,1)S(1)}, u32[]{:S(2)}, u32[]{:S(2)}) collective-permute-start(bf16[2,768,256]{2,1,0:T(8,128)(2,1)S(1)} %bitcast.25), channel_id=1, source_target_pairs={{0,4},{4,0},{1,5},{5,1},{2,6},{6,2},{3,7},{7,3},{8,12},{12,8},{9,1... | collective-permute-start | bytes 2359304 | tf_op jit(solution)/shard_map/ppermute | solution.py:462
  (74 shorter events, 27.7 us)
Async XLA Ops:
  0.6 8.3 %copy-start = (bf16[2,24,24,256]{3,2,1,0:T(8,128)(2,1)S(1)}, bf16[2,24,24,256]{3,2,1,0:T(8,128)(2,1)}, u32[]{:S(2)}) copy-start(bf16[2,24,24,256]{3,2,1,0:T(8,128)(2,1)} %param.29) | copy-start | bytes 1769476
  1.7 23.4 %collective-permute-start.25 = (bf16[96,728]{1,0:T(8,128)(2,1)S(1)}, bf16[96,728]{1,0:T(8,128)(2,1)S(1)}, u32[]{:S(2)}, u32[]{:S(2)}) collective-permute-start(bf16[96,728]{1,0:T(8,128)(2,1)S(1)} %get-tuple-element.161), channel_id=1, source_target_pairs={{1,2},{2,1},{3,4},{4,3},{5,6},{6,5},{7,8},{8,7},{9,10},{10,9},{11,... | collective-permute-start | bytes 419336 | tf_op jit(solution)/shard_map/ppermute | solution.py:50
  8.8 16.4 %collective-permute-start.24 = (bf16[96,728]{1,0:T(8,128)(2,1)S(1)}, bf16[96,728]{1,0:T(8,128)(2,1)S(1)}, u32[]{:S(2)}, u32[]{:S(2)}) collective-permute-start(bf16[96,728]{1,0:T(8,128)(2,1)S(1)} %get-tuple-element.162), channel_id=1, source_target_pairs={{0,1},{1,0},{2,3},{3,2},{4,5},{5,4},{6,7},{7,6},{8,9},{9,8},{10,11... | collective-permute-start | bytes 419336 | tf_op jit(solution)/shard_map/ppermute | solution.py:50
  9.6 14.8 %all-to-all-start = ((bf16[4,6,24,256]{3,2,1,0:T(8,128)(2,1)}), bf16[4,6,24,256]{3,2,1,0:T(8,128)(2,1)S(1)}, u32[]{:S(2)}, u32[]{:S(2)}) async-start(bf16[4,6,24,256]{3,2,1,0:T(8,128)(2,1)} %bitcast.2), calls=%async_computation | async-start | bytes 589824 | tf_op jit(solution)/shard_map/all_to_all | solution.py:482
  25.2 0.7 copy-start.10
  25.9 16.9 %copy-start.12 = (s32[2,2]{1,0:T(2,128)S(1)}, s32[2,2]{1,0:T(2,128)}, u32[]{:S(2)}) copy-start(s32[2,2]{1,0:T(2,128)} %sc_ref.8) | copy-start | bytes 52
  25.9 33.0 %copy-start.11 = (f32[2,9,256]{2,0,1:T(2,128)S(1)}, f32[2,9,256]{2,0,1:T(2,128)}, u32[]{:S(2)}) copy-start(f32[2,9,256]{2,0,1:T(2,128)} %param.35) | copy-start | bytes 55300
  37.1 8.6 %collective-permute-start.26 = (bf16[6,96,256]{2,1,0:T(8,128)(2,1)}, bf16[6,96,256]{2,1,0:T(8,128)(2,1)S(1)}, u32[]{:S(2)}, u32[]{:S(2)}) collective-permute-start(bf16[6,96,256]{2,1,0:T(8,128)(2,1)} %get-tuple-element.127.near_ref), channel_id=1, source_target_pairs={{0,1},{1,0},{2,3},{3,2},{4,5},{5,4},{6,7},{7,6},{8,9},{9,8},{10,11... | collective-permute-start | bytes 884744 | tf_op jit(solution)/shard_map/ppermute | solution.py:50
  38.5 11.4 %collective-permute-start.27 = (bf16[6,96,256]{2,1,0:T(8,128)(2,1)}, bf16[6,96,256]{2,1,0:T(8,128)(2,1)S(1)}, u32[]{:S(2)}, u32[]{:S(2)}) collective-permute-start(bf16[6,96,256]{2,1,0:T(8,128)(2,1)} %get-tuple-element.128.other_ref), channel_id=1, source_target_pairs={{1,2},{2,1},{3,4},{4,3},{5,6},{6,5},{7,8},{8,7},{9,10},{10,9},{11,... | collective-permute-start | bytes 884744 | tf_op jit(solution)/shard_map/ppermute | solution.py:50
  45.7 4.2 %copy-start.3 = (bf16[6,96,256]{2,1,0:T(8,128)(2,1)}, bf16[6,96,256]{2,1,0:T(8,128)(2,1)S(1)}, u32[]{:S(2)}) copy-start(bf16[6,96,256]{2,1,0:T(8,128)(2,1)S(1)} %collective-permute-done.26.of_near_ref) | copy-start | bytes 884740
  49.9 0.7 copy-start.4
  53.5 6.8 %collective-permute-start.29 = (bf16[1,3,96,256]{3,2,1,0:T(8,128)(2,1)}, bf16[1,3,96,256]{3,2,1,0:T(8,128)(2,1)S(1)}, u32[]{:S(2)}, u32[]{:S(2)}) collective-permute-start(bf16[1,3,96,256]{3,2,1,0:T(8,128)(2,1)} %bitcast.32), channel_id=1, source_target_pairs={{0,63},{1,2},{2,1},{3,4},{4,3},{5,6},{6,5},{7,8},{8,7},{9,10},{10,... | collective-permute-start | bytes 442376 | tf_op jit(solution)/shard_map/ppermute | solution.py:50
  57.0 4.7 %collective-permute-start.28 = (bf16[1,3,96,256]{3,2,1,0:T(8,128)(2,1)}, bf16[1,3,96,256]{3,2,1,0:T(8,128)(2,1)S(1)}, u32[]{:S(2)}, u32[]{:S(2)}) collective-permute-start(bf16[1,3,96,256]{3,2,1,0:T(8,128)(2,1)} %bitcast.31), channel_id=1, source_target_pairs={{0,1},{1,0},{2,3},{3,2},{4,5},{5,4},{6,7},{7,6},{8,9},{9,8},{10,11... | collective-permute-start | bytes 442376 | tf_op jit(solution)/shard_map/ppermute | solution.py:50
  60.2 1.5 copy-start.7
  63.9 10.3 %collective-permute-start.4 = (bf16[6,96,256]{2,1,0:T(8,128)(2,1)S(1)}, bf16[6,96,256]{2,1,0:T(8,128)(2,1)S(1)}, u32[]{:S(2)}, u32[]{:S(2)}) collective-permute-start(bf16[6,96,256]{2,1,0:T(8,128)(2,1)S(1)} %get-tuple-element.68), channel_id=1, source_target_pairs={{0,61},{1,62},{2,63},{3,0},{4,1},{5,2},{6,3},{7,4},{8,5},{9,6},{10... | collective-permute-start | bytes 884744 | tf_op jit(solution)/shard_map/cond/branch_3_fun/ppermute | solution.py:42
  64.3 9.9 %collective-permute-start.5 = (bf16[6,96,256]{2,1,0:T(8,128)(2,1)S(1)}, bf16[6,96,256]{2,1,0:T(8,128)(2,1)S(1)}, u32[]{:S(2)}, u32[]{:S(2)}) collective-permute-start(bf16[6,96,256]{2,1,0:T(8,128)(2,1)S(1)} %get-tuple-element.69), channel_id=1, source_target_pairs={{0,3},{1,4},{2,5},{3,6},{4,7},{5,8},{6,9},{7,10},{8,11},{9,12},{10... | collective-permute-start | bytes 884744 | tf_op jit(solution)/shard_map/cond/branch_3_fun/ppermute | solution.py:42
  74.3 10.5 %collective-permute-start.8 = (bf16[6,96,256]{2,1,0:T(8,128)(2,1)S(1)}, bf16[6,96,256]{2,1,0:T(8,128)(2,1)S(1)}, u32[]{:S(2)}, u32[]{:S(2)}) collective-permute-start(bf16[6,96,256]{2,1,0:T(8,128)(2,1)S(1)} %get-tuple-element.72), channel_id=1, source_target_pairs={{0,62},{1,63},{2,0},{3,1},{4,2},{5,3},{6,4},{7,5},{8,6},{9,7},{10,... | collective-permute-start | bytes 884744 | tf_op jit(solution)/shard_map/cond/branch_2_fun/ppermute | solution.py:42
  77.2 13.7 %collective-permute-start.9 = (bf16[6,96,256]{2,1,0:T(8,128)(2,1)S(1)}, bf16[6,96,256]{2,1,0:T(8,128)(2,1)S(1)}, u32[]{:S(2)}, u32[]{:S(2)}) collective-permute-start(bf16[6,96,256]{2,1,0:T(8,128)(2,1)S(1)} %get-tuple-element.73), channel_id=1, source_target_pairs={{0,2},{1,3},{2,4},{3,5},{4,6},{5,7},{6,8},{7,9},{8,10},{9,11},{10,... | collective-permute-start | bytes 884744 | tf_op jit(solution)/shard_map/cond/branch_2_fun/ppermute | solution.py:42
  95.6 9.2 %collective-permute-start.30 = (bf16[2,3,96,256]{3,2,1,0:T(8,128)(2,1)}, bf16[2,3,96,256]{3,2,1,0:T(8,128)(2,1)S(1)}, u32[]{:S(2)}, u32[]{:S(2)}) collective-permute-start(bf16[2,3,96,256]{3,2,1,0:T(8,128)(2,1)} %get-tuple-element.142), channel_id=1, source_target_pairs={{0,1},{1,0},{2,3},{3,2},{4,5},{5,4},{6,7},{7,6},{8,9},{9,8},{10,11... | collective-permute-start | bytes 884744 | tf_op jit(solution)/shard_map/ppermute | solution.py:50
  95.7 10.7 %collective-permute-start.31 = (bf16[2,3,96,256]{3,2,1,0:T(8,128)(2,1)}, bf16[2,3,96,256]{3,2,1,0:T(8,128)(2,1)S(1)}, u32[]{:S(2)}, u32[]{:S(2)}) collective-permute-start(bf16[2,3,96,256]{3,2,1,0:T(8,128)(2,1)} %get-tuple-element.143), channel_id=1, source_target_pairs={{0,63},{1,2},{2,1},{3,4},{4,3},{5,6},{6,5},{7,8},{8,7},{9,10},{10,... | collective-permute-start | bytes 884744 | tf_op jit(solution)/shard_map/ppermute | solution.py:50
  104.7 1.7 copy-start.5
  106.4 0.7 copy-start.6
  108.8 9.9 %collective-permute-start.16 = (bf16[6,96,256]{2,1,0:T(8,128)(2,1)S(1)}, bf16[6,96,256]{2,1,0:T(8,128)(2,1)S(1)}, u32[]{:S(2)}, u32[]{:S(2)}) collective-permute-start(bf16[6,96,256]{2,1,0:T(8,128)(2,1)S(1)} %get-tuple-element.80), channel_id=1, source_target_pairs={{0,61},{1,62},{2,63},{3,0},{4,1},{5,2},{6,3},{7,4},{8,5},{9,6},{10... | collective-permute-start | bytes 884744 | tf_op jit(solution)/shard_map/cond/branch_3_fun/ppermute | solution.py:42
  108.9 10.0 %collective-permute-start.17 = (bf16[6,96,256]{2,1,0:T(8,128)(2,1)S(1)}, bf16[6,96,256]{2,1,0:T(8,128)(2,1)S(1)}, u32[]{:S(2)}, u32[]{:S(2)}) collective-permute-start(bf16[6,96,256]{2,1,0:T(8,128)(2,1)S(1)} %get-tuple-element.81), channel_id=1, source_target_pairs={{0,3},{1,4},{2,5},{3,6},{4,7},{5,8},{6,9},{7,10},{8,11},{9,12},{10... | collective-permute-start | bytes 884744 | tf_op jit(solution)/shard_map/cond/branch_3_fun/ppermute | solution.py:42
  119.1 11.4 %collective-permute-start.20 = (bf16[6,96,256]{2,1,0:T(8,128)(2,1)S(1)}, bf16[6,96,256]{2,1,0:T(8,128)(2,1)S(1)}, u32[]{:S(2)}, u32[]{:S(2)}) collective-permute-start(bf16[6,96,256]{2,1,0:T(8,128)(2,1)S(1)} %get-tuple-element.84), channel_id=1, source_target_pairs={{0,62},{1,63},{2,0},{3,1},{4,2},{5,3},{6,4},{7,5},{8,6},{9,7},{10,... | collective-permute-start | bytes 884744 | tf_op jit(solution)/shard_map/cond/branch_2_fun/ppermute | solution.py:42
  125.2 11.7 %collective-permute-start.21 = (bf16[6,96,256]{2,1,0:T(8,128)(2,1)S(1)}, bf16[6,96,256]{2,1,0:T(8,128)(2,1)S(1)}, u32[]{:S(2)}, u32[]{:S(2)}) collective-permute-start(bf16[6,96,256]{2,1,0:T(8,128)(2,1)S(1)} %get-tuple-element.85), channel_id=1, source_target_pairs={{0,2},{1,3},{2,4},{3,5},{4,6},{5,7},{6,8},{7,9},{8,10},{9,11},{10,... | collective-permute-start | bytes 884744 | tf_op jit(solution)/shard_map/cond/branch_2_fun/ppermute | solution.py:42
  140.7 11.3 %collective-permute-start.33 = (bf16[6,96,256]{2,1,0:T(8,128)(2,1)}, bf16[6,96,256]{2,1,0:T(8,128)(2,1)S(1)}, u32[]{:S(2)}, u32[]{:S(2)}) collective-permute-start(bf16[6,96,256]{2,1,0:T(8,128)(2,1)} %gate.1.own_ref), channel_id=1, source_target_pairs={{1,2},{2,1},{3,4},{4,3},{5,6},{6,5},{7,8},{8,7},{9,10},{10,9},{11,... | collective-permute-start | bytes 884744 | tf_op jit(solution)/shard_map/ppermute | solution.py:50
  144.9 7.1 %collective-permute-start.32 = (bf16[6,96,256]{2,1,0:T(8,128)(2,1)}, bf16[6,96,256]{2,1,0:T(8,128)(2,1)S(1)}, u32[]{:S(2)}, u32[]{:S(2)}) collective-permute-start(bf16[6,96,256]{2,1,0:T(8,128)(2,1)} %gate.1.own_ref), channel_id=1, source_target_pairs={{0,1},{1,0},{2,3},{3,2},{4,5},{5,4},{6,7},{7,6},{8,9},{9,8},{10,11... | collective-permute-start | bytes 884744 | tf_op jit(solution)/shard_map/ppermute | solution.py:50
  152.0 0.7 copy-start.1
  152.0 0.8 copy-start.2
  161.6 2.5 %collective-permute-start.34 = (bf16[2,768,256]{2,1,0:T(8,128)(2,1)}, bf16[2,768,256]{2,1,0:T(8,128)(2,1)S(1)}, u32[]{:S(2)}, u32[]{:S(2)}) collective-permute-start(bf16[2,768,256]{2,1,0:T(8,128)(2,1)} %get-tuple-element.157), channel_id=1, source_target_pairs={{0,4},{4,0},{1,5},{5,1},{2,6},{6,2},{3,7},{7,3},{8,12},{12,8},{9,1... | collective-permute-start | bytes 2359304 | tf_op jit(solution)/shard_map/ppermute | solution.py:454
  207.5 5.0 %collective-permute-start.35 = (bf16[2,768,256]{2,1,0:T(8,128)(2,1)S(1)}, bf16[2,768,256]{2,1,0:T(8,128)(2,1)S(1)}, u32[]{:S(2)}, u32[]{:S(2)}) collective-permute-start(bf16[2,768,256]{2,1,0:T(8,128)(2,1)S(1)} %bitcast.25), channel_id=1, source_target_pairs={{0,4},{4,0},{1,5},{5,1},{2,6},{6,2},{3,7},{7,3},{8,12},{12,8},{9,1... | collective-permute-start | bytes 2359304 | tf_op jit(solution)/shard_map/ppermute | solution.py:462
  (2 other events, 1.3 us)
